TPU v7x, 512 devices: a whole 4x4x16 slice. The times are simulated.
512 devices in a mesh: dp: 32 (over z, x_lo), fsdp: 16 (over y, x_hi, core).
Axes of the slice: x: 4 (x_hi: 2, x_lo: 2; x = x_hi * 2 + x_lo), y: 4, z: 16, core: 2. Of those that a mesh axis runs over, the one named last changes fastest.
Arguments:
- images: bfloat16 [1024, 8, 8, 3072], P(('dp', 'fsdp')), may hold values from -6 to 6
- dw_weight: float32 [49, 3072], P(None, 'fsdp'), may hold values from -0.875 to 0.875
- dw_bias: float32 [3072], P('fsdp'), may hold values from -1 to 1
- block_gain: float32 [3072], P('fsdp'), may hold values from 0.5 to 1.5
- head_gain: float32 [3072], P('fsdp'), may hold values from 0.5 to 1.5
- projection: bfloat16 [3072, 512], P('fsdp'), may hold values from -0.109375 to 0.109375
- text: bfloat16 [1024, 512], P(('dp', 'fsdp')), may hold values from -6 to 6
Outputs:
- loss: float32 [], replicated
- grad_images: bfloat16 [1024, 8, 8, 3072], P(('dp', 'fsdp'))
- grad_dw_weight: float32 [49, 3072], P(None, 'fsdp')
- grad_dw_bias: float32 [3072], P('fsdp')
- grad_block_gain: float32 [3072], P('fsdp')
- grad_head_gain: float32 [3072], P('fsdp')
- grad_projection: float32 [3072, 512], P('fsdp')
- grad_text: float32 [1024, 512], P(('dp', 'fsdp'))
All inputs are finite; a program needn't handle non-finite values.
Results may differ from a plain program's by a relative error of at most 0.012.
Values may be sent and summed in bfloat16 or wider, within the bound.
A program may use at most 64 MiB of HBM per device.

v0:
```python
import jax
import jax.numpy as jnp
from jax import lax
from jax.sharding import PartitionSpec as P

KERNEL = 7
MAP_SIDE = 8


LOGIT_SCALE = 14.0
EPSILON = 1e-06


def depthwise(padded, weight):
    total = jnp.zeros(padded.shape[:1] + (MAP_SIDE, MAP_SIDE, padded.shape[3]), jnp.float32)
    for tap_row in range(KERNEL):
        for tap_col in range(KERNEL):
            window = padded[:, tap_row : tap_row + MAP_SIDE, tap_col : tap_col + MAP_SIDE, :]
            total = total + window * weight[tap_row * KERNEL + tap_col]
    return total


def contract(left, right, left_dim, right_dim):
    return lax.dot_general(
        left, right, (((left_dim,), (right_dim,)), ((), ())), preferred_element_type=jnp.float32
    )


def local(images, dw_weight, dw_bias, block_gain, head_gain, projection, text):
    full_weight, full_bias, full_block, full_head = (
        lax.all_gather(dw_weight, "fsdp", axis=1, tiled=True),
        lax.all_gather(dw_bias, "fsdp", axis=0, tiled=True),
        lax.all_gather(block_gain, "fsdp", axis=0, tiled=True),
        lax.all_gather(head_gain, "fsdp", axis=0, tiled=True),
    )
    margin = KERNEL // 2
    as_float = images.astype(jnp.float32)
    padded = jnp.pad(as_float, ((0, 0), (margin, margin), (margin, margin), (0, 0)))
    conv_out = depthwise(padded, full_weight) + full_bias
    centred = conv_out - jnp.mean(conv_out, axis=3, keepdims=True)
    inverse = lax.rsqrt(jnp.mean(centred * centred, axis=3, keepdims=True) + EPSILON)
    normal_z = centred * inverse
    hidden = as_float + normal_z * full_block
    pooled = jnp.mean(hidden, axis=(1, 2))
    pool_centred = pooled - jnp.mean(pooled, axis=1, keepdims=True)
    pool_inverse = lax.rsqrt(jnp.mean(pool_centred * pool_centred, axis=1, keepdims=True) + EPSILON)
    pool_normed = pool_centred * pool_inverse
    query = (pool_normed * full_head).astype(jnp.bfloat16)
    query_parts = lax.all_to_all(query, "fsdp", split_axis=1, concat_axis=0, tiled=True)
    panels = lax.all_gather(projection, "fsdp", axis=0, tiled=True)
    embedding = jnp.dot(query, panels, preferred_element_type=jnp.float32)
    image_scale = lax.rsqrt(jnp.sum(embedding * embedding, axis=1, keepdims=True) + EPSILON)
    image_f = embedding * image_scale
    image_unit = image_f.astype(jnp.bfloat16)
    text_float = text.astype(jnp.float32)
    text_scale = lax.rsqrt(jnp.sum(text_float * text_float, axis=1, keepdims=True) + EPSILON)
    text_f = text_float * text_scale
    text_unit = text_f.astype(jnp.bfloat16)
    image_all, text_all = (
        lax.all_gather(image_unit, ("dp", "fsdp"), axis=0, tiled=True),
        lax.all_gather(text_unit, ("dp", "fsdp"), axis=0, tiled=True),
    )
    local_count = images.shape[0]
    offset = lax.axis_index(("dp", "fsdp")) * local_count
    row_logits = LOGIT_SCALE * contract(image_unit, text_all, 1, 1)
    col_logits = LOGIT_SCALE * contract(image_all, text_unit, 1, 1)
    row_lse = jnp.log(jnp.sum(jnp.exp(row_logits), axis=1))
    col_lse = jnp.log(jnp.sum(jnp.exp(col_logits), axis=0))
    diagonal = LOGIT_SCALE * jnp.sum(
        image_unit.astype(jnp.float32) * text_unit.astype(jnp.float32), axis=1
    )
    every_row, every_col, every_diag = (
        lax.all_gather(row_lse, ("dp", "fsdp"), axis=0, tiled=True),
        lax.all_gather(col_lse, ("dp", "fsdp"), axis=0, tiled=True),
        lax.all_gather(diagonal, ("dp", "fsdp"), axis=0, tiled=True),
    )
    total_pairs = every_row.shape[0]
    loss = (jnp.sum(every_row) + jnp.sum(every_col) - 2.0 * jnp.sum(every_diag)) / (
        2.0 * total_pairs
    )
    positions = jnp.arange(total_pairs, dtype=jnp.int32)
    owners = offset + jnp.arange(local_count, dtype=jnp.int32)
    onehot = (positions[None, :] == owners[:, None]).astype(jnp.float32)
    row_weights = (
        jnp.exp(row_logits - row_lse[:, None])
        + jnp.exp(row_logits - every_col[None, :])
        - 2.0 * onehot
    ).astype(jnp.bfloat16)
    col_weights = (
        jnp.exp(col_logits - every_row[:, None])
        + jnp.exp(col_logits - col_lse[None, :])
        - 2.0 * onehot.T
    ).astype(jnp.bfloat16)
    d_image = 7.0 * jnp.dot(row_weights, text_all, preferred_element_type=jnp.float32)
    d_caption = 7.0 * contract(col_weights, image_all, 0, 0)
    d_embedding = (
        image_scale * (d_image - image_f * jnp.sum(image_f * d_image, axis=1, keepdims=True))
    ).astype(jnp.bfloat16)
    grad_text = text_scale * (
        d_caption - text_f * jnp.sum(text_f * d_caption, axis=1, keepdims=True)
    )
    demb_group = lax.all_gather(d_embedding, "fsdp", axis=0, tiled=True)
    proj_grad = contract(query_parts, demb_group, 0, 0)
    d_query = contract(d_embedding, panels, 1, 1)
    d_normed = d_query * full_head
    g_head = jnp.sum(d_query * pool_normed, axis=0)
    d_pooled = pool_inverse * (
        d_normed
        - jnp.mean(d_normed, axis=1, keepdims=True)
        - pool_normed * jnp.mean(d_normed * pool_normed, axis=1, keepdims=True)
    )
    d_hidden = (d_pooled / float(MAP_SIDE * MAP_SIDE))[:, None, None, :]
    d_norm = d_hidden * full_block
    g_block = jnp.sum(d_hidden * normal_z, axis=(0, 1, 2))
    d_conv = inverse * (
        d_norm
        - jnp.mean(d_norm, axis=3, keepdims=True)
        - normal_z * jnp.mean(d_norm * normal_z, axis=3, keepdims=True)
    )
    g_bias = jnp.sum(d_conv, axis=(0, 1, 2))
    d_padded = jnp.pad(d_conv, ((0, 0), (margin, margin), (margin, margin), (0, 0)))
    tap_grads = []
    d_images = d_hidden + jnp.zeros_like(d_conv)
    for tap_row in range(KERNEL):
        for tap_col in range(KERNEL):
            window = padded[:, tap_row : tap_row + MAP_SIDE, tap_col : tap_col + MAP_SIDE, :]
            tap_grads.append(jnp.sum(d_conv * window, axis=(0, 1, 2)))
            back = d_padded[
                :,
                2 * margin - tap_row : 2 * margin - tap_row + MAP_SIDE,
                2 * margin - tap_col : 2 * margin - tap_col + MAP_SIDE,
                :,
            ]
            d_images = d_images + back * full_weight[tap_row * KERNEL + tap_col]
    g_weight = jnp.stack(tap_grads)
    part_weight, part_bias, part_block, part_head = (
        lax.psum_scatter(g_weight, "fsdp", scatter_dimension=1, tiled=True),
        lax.psum_scatter(g_bias, "fsdp", scatter_dimension=0, tiled=True),
        lax.psum_scatter(g_block, "fsdp", scatter_dimension=0, tiled=True),
        lax.psum_scatter(g_head, "fsdp", scatter_dimension=0, tiled=True),
    )
    sum_weight, sum_bias, sum_block, sum_head, sum_proj = lax.psum(
        (part_weight, part_bias, part_block, part_head, proj_grad), "dp"
    )
    return (
        loss,
        d_images.astype(jnp.bfloat16),
        sum_weight,
        sum_bias,
        sum_block,
        sum_head,
        sum_proj,
        grad_text,
    )


def solution(mesh):
    return jax.shard_map(
        local,
        mesh=mesh,
        in_specs=(
            P(("dp", "fsdp"), None, None, None),
            P(None, "fsdp"),
            P("fsdp"),
            P("fsdp"),
            P("fsdp"),
            P("fsdp", None),
            P(("dp", "fsdp"), None),
        ),
        out_specs=(
            P(),
            P(("dp", "fsdp"), None, None, None),
            P(None, "fsdp"),
            P("fsdp"),
            P("fsdp"),
            P("fsdp"),
            P("fsdp", None),
            P(("dp", "fsdp"), None),
        ),
        check_vma=False,
    )
```

profile of v0, /device:TPU:6, one launch (start us, length us, event | category | flops | bytes accessed | tf_op | source)
XLA Modules:
  0.0 2227.8 jit_solution(11575561516436154558)
XLA Ops:
  7.2 0.7 all-gather.8.cloned.1.call-update
  8.0 24.1 %all-gather = f32[16,192,49]{1,2,0:T(8,128)S(1)} all-gather(f32[1,192,49]{1,2,0:T(8,128)} %bitcast.227), channel_id=1, replica_groups=mesh['dp'=32,'fsdp'=16] {'fsdp'}, dimensions={0}, use_global_device_ids=true | all-gather | bytes 639744 | tf_op jit(solution)/shard_map/all_gather | solution.py:31
  32.4 1.2 reshape.181
  35.9 65.1 %all-reduce.14 = (f32[3072]{0:T(1024)}, f32[3072]{0:T(1024)}, f32[3072]{0:T(1024)S(1)}) all-reduce(f32[3072]{0:T(1024)S(1)} %dynamic-update-slice, f32[3072]{0:T(1024)S(1)} %dynamic-update-slice.1, f32[3072]{0:T(1024)S(1)} %dynamic-update-slice.2), channel_id=1, replica_groups=mesh['dp'=32,'fsdp'=16] {'fsdp'}, use_global_device_ids=true, to_apply=%add.2 | all-reduce | flops 9216 | bytes 73728
  101.8 14.5 fusion.131
  116.9 0.8 copy-done.3
  118.1 0.7 broadcast_multiply_fusion.2
  119.1 2.6 multiply_reduce_fusion.58
  121.7 1.3 multiply_reduce_fusion.57
  123.1 0.7 all-gather.10.cloned.1.call-update
  123.8 0.7 mul.1444
  124.5 0.8 div.46
  125.3 0.8 multiply_convert_fusion
  126.1 0.6 copy.22
  126.7 9.2 all-to-all-start
  135.9 1.3 broadcast_multiply_fusion.3
  138.4 2.3 all-to-all-done
  140.7 0.6 all_to_all.14
  141.3 0.7 multiply_dynamic-update-slice_fusion
  142.0 751.1 %all-gather.12.cloned.1.call-done = bf16[512,2,512]{2,1,0:T(2,128)(2,1)} async-done(((bf16[1,2,512]{2,1,0:T(2,128)(2,1)}), bf16[512,2,512]{2,1,0:T(2,128)(2,1)}) %all-gather.12.cloned.1.call-update) | async-done | bytes 1048592 | tf_op jit(solution)/shard_map/all_gather | solution.py:60
  893.1 2.3 reshape.185
  895.4 2.3 exponential_reduce_fusion
  897.7 756.1 %all-gather.10.cloned.1.call-done = bf16[512,2,512]{2,1,0:T(2,128)(2,1)} async-done(((bf16[1,2,512]{2,1,0:T(2,128)(2,1)}), bf16[512,2,512]{2,1,0:T(2,128)(2,1)}) %all-gather.10.cloned.1.call-update) | async-done | bytes 1048592 | tf_op jit(solution)/shard_map/all_gather | solution.py:61
  1653.8 2.3 reshape.183
  1656.1 1.7 exponential_reduce_fusion.1
  1658.9 101.8 %all-reduce.11 = (f32[1024]{0:T(1024)}, f32[1024]{0:T(1024)S(1)}, f32[1024]{0:T(1024)}) all-reduce(f32[1024]{0:T(1024)S(1)} %get-tuple-element.153, f32[1024]{0:T(1024)S(1)} %get-tuple-element.151, f32[1024]{0:T(1024)S(1)} %multiply_dynamic-update-slice_fusion), channel_id=1, replica_groups=mesh['dp'=32,'fsdp'=16] {'dp','fsdp'}, use_global_device_ids=true, to_apply=%add.5 | all-reduce | flops 3072 | bytes 24576
  1760.7 1.7 multiply_reduce_fusion.56
  1762.4 0.7 multiply_convert_fusion.3
  1763.1 3.4 multiply_reduce_fusion.52
  1766.9 1.1 multiply_reduce_fusion
  1768.0 4.7 multiply_reduce_fusion.1
  1772.7 2.4 fusion.128
  1775.3 3.8 multiply_reduce_fusion.19
  1779.1 20.5 all-gather.3
  1799.7 62.4 %all-reduce.13 = (f32[3072]{0:T(1024)S(1)}, f32[3072]{0:T(1024)S(1)}, f32[3072]{0:T(1024)S(1)}) all-reduce(f32[3072]{0:T(1024)S(1)} %get-tuple-element.58, f32[3072]{0:T(1024)S(1)} %copy-done.73, f32[3072]{0:T(1024)S(1)} %copy-done.72), channel_id=3, replica_groups=mesh['dp'=32,'fsdp'=16] {'fsdp'}, use_global_device_ids=true, to_apply=%region_70.71.clone | all-reduce | flops 9216 | bytes 73728
  1862.5 0.9 stack.199
  1863.4 1.7 copy.23
  1865.3 1.4 reduce_sum.649
  1866.8 1.0 fusion.138
  1868.1 9.5 fusion.97
  1877.6 0.6 reduce_sum.647
  1879.5 0.6 reduce_sum.651
  1881.2 0.7 fusion.115
  1881.9 70.7 %reduce-scatter.4.cloned.1.call-done = f32[192,49]{1,0:T(8,128)} async-done(((f32[3072,49]{1,0:T(8,128)}), f32[192,49]{1,0:T(8,128)}) %reduce-scatter.4.cloned.1.call-update) | async-done | bytes 37648
  1952.7 1.0 copy.24
  1953.6 119.5 %all-reduce.12 = (f32[49,192]{1,0:T(8,128)}, f32[192]{0:T(256)}, f32[192]{0:T(256)}, f32[192]{0:T(256)}) all-reduce(f32[49,192]{1,0:T(8,128)S(1)} %copy.24, f32[192]{0:T(256)S(1)} %dynamic-slice.4, f32[192]{0:T(256)S(1)} %dynamic-slice.6, f32[192]{0:T(256)S(1)} %dynamic-slice.8), channel_id=1, replica_groups=mesh['dp'=32,'fsdp'=16] {'dp'}, use_global_device_ids=true, to_apply=%region_68.69 | all-reduce | flops 9984 | bytes 79872 | tf_op jit(solution)/shard_map/psum | solution.py:142
  2073.1 145.2 %all-reduce.17.cloned.1.call-done = f32[192,512]{1,0:T(8,128)} async-done(((f32[192,512]{1,0:T(8,128)}), f32[192,512]{1,0:T(8,128)}) %all-reduce.17.cloned.1.call-update) | async-done | bytes 393232 | tf_op jit(solution)/shard_map/psum | solution.py:142
  2218.3 1.8 copy.35
  (239 shorter events, 6.6 us)
Async XLA Ops:
  7.2 112.0 %all-gather.8.cloned.1.call-start = ((), (), s32[]{:S(2)}) async-start(), calls=%async_computation.2 | async-start | bytes 3342336 | tf_op jit(solution)/shard_map/all_gather | solution.py:50
  7.9 885.2 %all-gather.12.cloned.1.call-start = ((), (), s32[]{:S(2)}) async-start(), calls=%async_computation.5 | async-start | bytes 1050624 | tf_op jit(solution)/shard_map/all_gather | solution.py:60
  33.6 67.4 %copy-start.77 = (bf16[2,512]{1,0:T(2,128)(2,1)S(1)}, bf16[2,512]{1,0:T(2,128)(2,1)}, u32[]{:S(2)}) copy-start(bf16[2,512]{1,0:T(2,128)(2,1)} %param.13) | copy-start | bytes 6148
  33.6 67.5 %copy-start.6 = (f32[3072,49]{0,1:T(8,128)S(1)}, f32[3072,49]{0,1:T(8,128)}, u32[]{:S(2)}) copy-start(f32[3072,49]{0,1:T(8,128)} %reshape.181) | copy-start | bytes 1806340
  101.4 14.9 copy-start.7
  101.4 14.9 copy-start.9
  101.4 14.9 copy-start.11
  101.4 14.9 copy-start.13
  101.6 14.7 copy-start.15
  101.6 14.7 copy-start.17
  101.6 14.7 copy-start.19
  101.6 14.7 copy-start.21
  101.6 14.7 copy-start.23
  101.6 14.7 copy-start.25
  101.6 14.7 copy-start.27
  101.7 14.7 copy-start.29
  101.7 14.7 copy-start.31
  101.7 14.7 copy-start.33
  101.7 14.7 copy-start.35
  101.7 14.7 copy-start.37
  101.7 14.7 copy-start.39
  123.0 1530.8 %all-gather.10.cloned.1.call-start = ((), (), s32[]{:S(2)}) async-start(), calls=%async_computation.4 | async-start | bytes 1050624 | tf_op jit(solution)/shard_map/all_gather | solution.py:61
  126.1 769.3 %copy-start.76 = (bf16[2,512]{1,0:T(2,128)(2,1)S(1)}, bf16[2,512]{1,0:T(2,128)(2,1)}, u32[]{:S(2)}) copy-start(bf16[2,512]{1,0:T(2,128)(2,1)} %get-tuple-element.93) | copy-start | bytes 6148
  126.7 14.0 all-to-all-start
  135.9 1816.8 %reduce-scatter.4.cloned.1.call-start = ((), (), s32[]{:S(2)}) async-start(), calls=%async_computation.6 | async-start | bytes 1671168
  895.4 760.7 %copy-start.75 = (bf16[2,512]{1,0:T(2,128)(2,1)S(1)}, bf16[2,512]{1,0:T(2,128)(2,1)}, u32[]{:S(2)}) copy-start(bf16[2,512]{1,0:T(2,128)(2,1)} %get-tuple-element.94) | copy-start | bytes 6148
  1656.1 107.0 %copy-start.80 = (f32[2]{0:T(128)S(1)}, f32[2]{0:T(128)}, u32[]{:S(2)}) copy-start(f32[2]{0:T(128)} %copy-done.79) | copy-start | bytes 28
  1656.1 107.0 %copy-start.83 = (f32[2]{0:T(128)S(1)}, f32[2]{0:T(128)}, u32[]{:S(2)}) copy-start(f32[2]{0:T(128)} %copy-done.82) | copy-start | bytes 28
  1775.1 24.6 %copy-start.72 = (f32[3072]{0:T(1024)S(1)}, f32[3072]{0:T(1024)}, u32[]{:S(2)}) copy-start(f32[3072]{0:T(1024)} %get-tuple-element.72) | copy-start | bytes 36868
  1775.1 24.6 %copy-start.73 = (f32[3072]{0:T(1024)S(1)}, f32[3072]{0:T(1024)}, u32[]{:S(2)}) copy-start(f32[3072]{0:T(1024)} %get-tuple-element.56) | copy-start | bytes 36868
  1775.1 87.2 %copy-start.54 = (f32[3072]{0:T(1024)S(1)}, f32[3072]{0:T(1024)}, u32[]{:S(2)}) copy-start(f32[3072]{0:T(1024)} %get-tuple-element.9) | copy-start | bytes 36868
  1775.1 87.2 %copy-start.55 = (f32[3072]{0:T(1024)S(1)}, f32[3072]{0:T(1024)}, u32[]{:S(2)}) copy-start(f32[3072]{0:T(1024)} %get-tuple-element.10) | copy-start | bytes 36868
  1775.1 87.2 %copy-start.56 = (f32[3072]{0:T(1024)S(1)}, f32[3072]{0:T(1024)}, u32[]{:S(2)}) copy-start(f32[3072]{0:T(1024)} %get-tuple-element.11) | copy-start | bytes 36868
  1775.1 87.2 %copy-start.57 = (f32[3072]{0:T(1024)S(1)}, f32[3072]{0:T(1024)}, u32[]{:S(2)}) copy-start(f32[3072]{0:T(1024)} %get-tuple-element.12) | copy-start | bytes 36868
  1775.2 87.2 %copy-start.58 = (f32[3072]{0:T(1024)S(1)}, f32[3072]{0:T(1024)}, u32[]{:S(2)}) copy-start(f32[3072]{0:T(1024)} %get-tuple-element.13) | copy-start | bytes 36868
  1775.2 87.2 %copy-start.59 = (f32[3072]{0:T(1024)S(1)}, f32[3072]{0:T(1024)}, u32[]{:S(2)}) copy-start(f32[3072]{0:T(1024)} %get-tuple-element.14) | copy-start | bytes 36868
  1775.2 87.2 %copy-start.60 = (f32[3072]{0:T(1024)S(1)}, f32[3072]{0:T(1024)}, u32[]{:S(2)}) copy-start(f32[3072]{0:T(1024)} %get-tuple-element.15) | copy-start | bytes 36868
  1775.2 87.2 %copy-start.61 = (f32[3072]{0:T(1024)S(1)}, f32[3072]{0:T(1024)}, u32[]{:S(2)}) copy-start(f32[3072]{0:T(1024)} %get-tuple-element.16) | copy-start | bytes 36868
  1775.2 87.2 %copy-start.62 = (f32[3072]{0:T(1024)S(1)}, f32[3072]{0:T(1024)}, u32[]{:S(2)}) copy-start(f32[3072]{0:T(1024)} %get-tuple-element.17) | copy-start | bytes 36868
  1775.2 87.2 %copy-start.63 = (f32[3072]{0:T(1024)S(1)}, f32[3072]{0:T(1024)}, u32[]{:S(2)}) copy-start(f32[3072]{0:T(1024)} %get-tuple-element.18) | copy-start | bytes 36868
  1775.2 87.2 %copy-start.64 = (f32[3072]{0:T(1024)S(1)}, f32[3072]{0:T(1024)}, u32[]{:S(2)}) copy-start(f32[3072]{0:T(1024)} %get-tuple-element.19) | copy-start | bytes 36868
  1775.2 87.2 %copy-start.65 = (f32[3072]{0:T(1024)S(1)}, f32[3072]{0:T(1024)}, u32[]{:S(2)}) copy-start(f32[3072]{0:T(1024)} %get-tuple-element.20) | copy-start | bytes 36868
  1775.2 87.2 %copy-start.66 = (f32[3072]{0:T(1024)S(1)}, f32[3072]{0:T(1024)}, u32[]{:S(2)}) copy-start(f32[3072]{0:T(1024)} %get-tuple-element.21) | copy-start | bytes 36868
  1775.2 87.2 %copy-start.67 = (f32[3072]{0:T(1024)S(1)}, f32[3072]{0:T(1024)}, u32[]{:S(2)}) copy-start(f32[3072]{0:T(1024)} %get-tuple-element.22) | copy-start | bytes 36868
  1775.3 87.2 %copy-start.68 = (f32[3072]{0:T(1024)S(1)}, f32[3072]{0:T(1024)}, u32[]{:S(2)}) copy-start(f32[3072]{0:T(1024)} %get-tuple-element.23) | copy-start | bytes 36868
  1775.3 87.2 %copy-start.69 = (f32[3072]{0:T(1024)S(1)}, f32[3072]{0:T(1024)}, u32[]{:S(2)}) copy-start(f32[3072]{0:T(1024)} %get-tuple-element.24) | copy-start | bytes 36868
  1775.3 87.2 %copy-start.70 = (f32[3072]{0:T(1024)S(1)}, f32[3072]{0:T(1024)}, u32[]{:S(2)}) copy-start(f32[3072]{0:T(1024)} %get-tuple-element.25) | copy-start | bytes 36868
  1865.3 353.0 %all-reduce.17.cloned.1.call-start = ((), (), s32[]{:S(2)}) async-start(), calls=%async_computation.3 | async-start | bytes 786432 | tf_op jit(solution)/shard_map/psum | solution.py:142
  (54 other events, 289.2 us)
Sparse Core Ops, SparseCore 0:
  11.3 68.9 all-gather.7
  123.2 769.8 all-gather.11
  895.8 757.9 all-gather.9
  1865.4 87.1 reduce-scatter.3
  1956.0 262.3 all-reduce.16
where the time goes:
time: 2230 us
  waiting for transfers between devices  1730 us (78%)
  blocking collectives  393 us (18%)
  other arithmetic  47 us (2%)
    all_gather x1, waiting for transfers between devices, local(): lax.all_gather(text_unit, ('dp', 'fsdp'), axis=0, tiled=True)  756 us
    all_gather x1, waiting for transfers between devices, local(): lax.all_gather(image_unit, ('dp', 'fsdp'), axis=0, tiled=True)  751 us
    unnamed x3, blocking collectives  229 us
    psum x1, waiting for transfers between devices, local(): lax.psum((part_weight, part_bias, part_block, part_head, proj_grad), 'dp')  145 us
    psum x1, blocking collectives, local(): lax.psum((part_weight, part_bias, part_block, part_head, proj_grad), 'dp')  119 us
    unnamed x6, waiting for transfers between devices  72.2 us
  transfers between devices with their start and end apart: 6, of which 5 were waited for; matrix products, arithmetic and copies ran while one was open for 2% of the time, Pallas kernels for 0%

commit v1 on v0

v1 whole, which is shorter than its diff:
```python
import jax
import jax.numpy as jnp
from jax import lax
from jax.sharding import PartitionSpec as P

KERNEL = 7
MAP_SIDE = 8


LOGIT_SCALE = 14.0
EPSILON = 1e-06


def depthwise(padded, weight):
    total = jnp.zeros(padded.shape[:1] + (MAP_SIDE, MAP_SIDE, padded.shape[3]), jnp.float32)
    for tap_row in range(KERNEL):
        for tap_col in range(KERNEL):
            window = padded[:, tap_row : tap_row + MAP_SIDE, tap_col : tap_col + MAP_SIDE, :]
            total = total + window * weight[tap_row * KERNEL + tap_col]
    return total


def contract(left, right, left_dim, right_dim):
    return lax.dot_general(
        left, right, (((left_dim,), (right_dim,)), ((), ())), preferred_element_type=jnp.float32
    )


N_DP = 32
N_FSDP = 16


def share(value, axis, count):
    return lax.all_to_all(
        jnp.broadcast_to(value[None], (count,) + value.shape), axis, split_axis=0, concat_axis=0, tiled=True
    )


def swap(blocks, axis):
    return lax.all_to_all(blocks, axis, split_axis=0, concat_axis=0, tiled=True)


def local(images, dw_weight, dw_bias, block_gain, head_gain, projection, text):
    channels = images.shape[3]
    shard = dw_bias.shape[0]
    count = images.shape[0]
    embed = text.shape[1]
    pack = jnp.concatenate([dw_weight, dw_bias[None], block_gain[None]], axis=0)
    pack_all = share(pack, "fsdp", N_FSDP).transpose(1, 0, 2).reshape(pack.shape[0], channels)
    full_weight, full_bias, full_block = pack_all[:49], pack_all[49], pack_all[50]
    text_float = text.astype(jnp.float32)
    text_scale = lax.rsqrt(jnp.sum(text_float * text_float, axis=1, keepdims=True) + EPSILON)
    text_f = text_float * text_scale
    text_unit = text_f.astype(jnp.bfloat16)
    text_cols = share(text_unit, "dp", N_DP).reshape(N_DP * count, embed)

    margin = KERNEL // 2
    as_float = images.astype(jnp.float32)
    padded = jnp.pad(as_float, ((0, 0), (margin, margin), (margin, margin), (0, 0)))
    conv_out = depthwise(padded, full_weight) + full_bias
    centred = conv_out - jnp.mean(conv_out, axis=3, keepdims=True)
    inverse = lax.rsqrt(jnp.mean(centred * centred, axis=3, keepdims=True) + EPSILON)
    normal_z = centred * inverse
    hidden = as_float + normal_z * full_block
    pooled = jnp.mean(hidden, axis=(1, 2))
    pool_centred = pooled - jnp.mean(pooled, axis=1, keepdims=True)
    pool_inverse = lax.rsqrt(jnp.mean(pool_centred * pool_centred, axis=1, keepdims=True) + EPSILON)
    pool_normed = pool_centred * pool_inverse

    normed_group = swap(
        pool_normed.reshape(count, N_FSDP, shard).transpose(1, 0, 2), "fsdp"
    ).reshape(N_FSDP * count, shard)
    query_group = (normed_group * head_gain).astype(jnp.bfloat16)
    part = jnp.dot(query_group, projection, preferred_element_type=jnp.float32)
    embedding = jnp.sum(swap(part.reshape(N_FSDP, count, embed), "fsdp"), axis=0)
    image_scale = lax.rsqrt(jnp.sum(embedding * embedding, axis=1, keepdims=True) + EPSILON)
    image_f = embedding * image_scale
    image_unit = image_f.astype(jnp.bfloat16)
    image_rows = share(image_unit, "fsdp", N_FSDP).reshape(N_FSDP * count, embed)

    logits = LOGIT_SCALE * contract(image_rows, text_cols, 1, 1)
    exps = jnp.exp(logits)
    row_lse = jnp.log(jnp.sum(share(jnp.sum(exps, axis=1), "fsdp", N_FSDP), axis=0))
    col_lse = jnp.log(jnp.sum(share(jnp.sum(exps, axis=0), "dp", N_DP), axis=0))
    group = lax.axis_index("dp")
    member = lax.axis_index("fsdp")
    rows = jnp.arange(N_FSDP * count, dtype=jnp.int32)[:, None]
    cols = jnp.arange(N_DP * count, dtype=jnp.int32)[None, :]
    same = (
        (rows // count == member) & (cols // count == group) & (rows % count == cols % count)
    ).astype(jnp.float32)
    diagonal = LOGIT_SCALE * jnp.sum(
        image_unit.astype(jnp.float32) * text_unit.astype(jnp.float32), axis=1
    )
    loss_part = (
        jnp.sum(row_lse) / N_FSDP + jnp.sum(col_lse) / N_DP - 2.0 * jnp.sum(diagonal)
    )
    weights = (
        jnp.exp(logits - row_lse[:, None]) + jnp.exp(logits - col_lse[None, :]) - 2.0 * same
    ).astype(jnp.bfloat16)
    d_image = 7.0 * jnp.sum(
        swap(
            jnp.dot(weights, text_cols, preferred_element_type=jnp.float32).reshape(
                N_FSDP, count, embed
            ),
            "fsdp",
        ),
        axis=0,
    )
    d_embedding = (
        image_scale * (d_image - image_f * jnp.sum(image_f * d_image, axis=1, keepdims=True))
    ).astype(jnp.bfloat16)
    d_caption = 7.0 * jnp.sum(
        swap(contract(weights, image_rows, 0, 0).reshape(N_DP, count, embed), "dp"), axis=0
    )
    grad_text = text_scale * (
        d_caption - text_f * jnp.sum(text_f * d_caption, axis=1, keepdims=True)
    )
    demb_group = share(d_embedding, "fsdp", N_FSDP).reshape(N_FSDP * count, embed)
    proj_grad = contract(query_group, demb_group, 0, 0)
    d_query = contract(demb_group, projection, 1, 1)
    g_head = jnp.sum(d_query * normed_group, axis=0)
    d_normed = (
        swap((d_query * head_gain).reshape(N_FSDP, count, shard), "fsdp")
        .transpose(1, 0, 2)
        .reshape(count, channels)
    )
    d_pooled = pool_inverse * (
        d_normed
        - jnp.mean(d_normed, axis=1, keepdims=True)
        - pool_normed * jnp.mean(d_normed * pool_normed, axis=1, keepdims=True)
    )
    d_hidden = (d_pooled / float(MAP_SIDE * MAP_SIDE))[:, None, None, :]
    d_norm = d_hidden * full_block
    g_block = jnp.sum(d_hidden * normal_z, axis=(0, 1, 2))
    d_conv = inverse * (
        d_norm
        - jnp.mean(d_norm, axis=3, keepdims=True)
        - normal_z * jnp.mean(d_norm * normal_z, axis=3, keepdims=True)
    )
    g_bias = jnp.sum(d_conv, axis=(0, 1, 2))
    d_padded = jnp.pad(d_conv, ((0, 0), (margin, margin), (margin, margin), (0, 0)))
    tap_grads = []
    d_images = d_hidden + jnp.zeros_like(d_conv)
    for tap_row in range(KERNEL):
        for tap_col in range(KERNEL):
            window = padded[:, tap_row : tap_row + MAP_SIDE, tap_col : tap_col + MAP_SIDE, :]
            tap_grads.append(jnp.sum(d_conv * window, axis=(0, 1, 2)))
            back = d_padded[
                :,
                2 * margin - tap_row : 2 * margin - tap_row + MAP_SIDE,
                2 * margin - tap_col : 2 * margin - tap_col + MAP_SIDE,
                :,
            ]
            d_images = d_images + back * full_weight[tap_row * KERNEL + tap_col]
    grads = jnp.stack(tap_grads + [g_bias, g_block, jnp.full((channels,), loss_part)])
    held = jnp.sum(
        swap(grads.reshape(52, N_FSDP, shard).transpose(1, 0, 2), "fsdp"), axis=0
    )
    small = jnp.concatenate([held, g_head[None], jnp.zeros((11, shard), jnp.float32)])
    both = jnp.concatenate(
        [small.reshape(N_DP, 2 * shard), proj_grad.reshape(N_DP, shard // N_DP * embed)], axis=1
    )
    total = share(jnp.sum(swap(both[:, None], "dp"), axis=0), "dp", N_DP).reshape(both.shape)
    sums = total[:, : 2 * shard].reshape(64, shard)
    sum_proj = total[:, 2 * shard :].reshape(shard, embed)
    pairs = N_DP * N_FSDP * count
    return (
        sums[51, 0] / (2.0 * pairs),
        d_images.astype(jnp.bfloat16),
        sums[:49],
        sums[49],
        sums[50],
        sums[52],
        sum_proj,
        grad_text,
    )


def solution(mesh):
    return jax.shard_map(
        local,
        mesh=mesh,
        in_specs=(
            P(("dp", "fsdp"), None, None, None),
            P(None, "fsdp"),
            P("fsdp"),
            P("fsdp"),
            P("fsdp"),
            P("fsdp", None),
            P(("dp", "fsdp"), None),
        ),
        out_specs=(
            P(),
            P(("dp", "fsdp"), None, None, None),
            P(None, "fsdp"),
            P("fsdp"),
            P("fsdp"),
            P("fsdp"),
            P("fsdp", None),
            P(("dp", "fsdp"), None),
        ),
        check_vma=False,
    )
```

time: 2230 us -> 354 us (0.16)
  waiting for transfers between devices: 1730 us -> 126 us
  blocking collectives: 393 us -> 21 us
  starting transfers between devices: 9.36 us -> 77.8 us
  local copies, waits for them, and re-layouts: 18.4 us -> 56.3 us
    all_gather x3 -> x0, waiting for transfers between devices: 1510 us -> none  [the longest x1 756 us: local(): lax.all_gather(text_unit, ('dp', 'fsdp'), axis=0, tiled=True)]
    unnamed x3 -> x0, blocking collectives: 229 us -> none
    psum x1 -> x0, waiting for transfers between devices: 145 us -> none  [local(): lax.psum((part_weight, part_bias, part_block, part_head, proj_grad), 'dp')]
    all_to_all x1 -> x12, waiting for transfers between devices: 2.27 us -> 126 us  [the longest x6 68.2 us: swap(): return lax.all_to_all(blocks, axis, split_axis=0, concat_axis=0, tiled=True)]
    psum x1 -> x0, blocking collectives: 119 us -> none  [local(): lax.psum((part_weight, part_bias, part_block, part_head, proj_grad), 'dp')]
    unnamed x6 -> x0, waiting for transfers between devices: 72.2 us -> none
    all_to_all x1 -> x12, starting transfers between devices: 9.17 us -> 77.8 us  [the longest x6 44.7 us: share(): lax.all_to_all(jnp.broadcast_to(value[None], (count,) + value.shape), axi...]
    all_gather x2 -> x0, blocking collectives: 44.6 us -> none  [the longest x1 24.1 us: local(): lax.all_gather(dw_weight, 'fsdp', axis=1, tiled=True)]
  transfers between devices with their start and end apart: 6 -> 12, of which waited for: 5 -> 12; matrix products, arithmetic and copies ran while one was open for 2% -> 7% of each run, Pallas kernels for 0% -> 0%
where the time goes in v1:
time: 354 us; the launch traced here: 352 us
  waiting for transfers between devices  126 us (36%)
  starting transfers between devices  77.8 us (22%)
  other arithmetic  59.4 us (17%)
  local copies, waits for them, and re-layouts  56.3 us (16%)
  blocking collectives  21 us (6%)
  between operations  5.89 us (2%)
  matrix products  5.1 us (1%)
    all_to_all x6, waiting for transfers between devices, swap(): return lax.all_to_all(blocks, axis, split_axis=0, concat_axis=0, tiled=True)  68.2 us
    all_to_all x6, waiting for transfers between devices, share(): lax.all_to_all(jnp.broadcast_to(value[None], (count,) + value.shape), axi...  57.8 us
    all_to_all x6, starting transfers between devices, share(): lax.all_to_all(jnp.broadcast_to(value[None], (count,) + value.shape), axi...  44.7 us
    all_to_all x6, starting transfers between devices, swap(): return lax.all_to_all(blocks, axis, split_axis=0, concat_axis=0, tiled=True)  33.1 us
    mul x49, local copies, waits for them, and re-layouts, depthwise(): total = total + window * weight[tap_row * KERNEL + tap_col]  24.1 us
    reduce_sum x1, other arithmetic, local(): centred = conv_out - jnp.mean(conv_out, axis=3, keepdims=True)  15.5 us
    all_to_all x1, blocking collectives, swap(): return lax.all_to_all(blocks, axis, split_axis=0, concat_axis=0, tiled=True)  10.9 us
    convert_element_type x1, other arithmetic, local(): d_images.astype(jnp.bfloat16)  10.6 us
  transfers between devices with their start and end apart: 12, of which 12 were waited for; matrix products, arithmetic and copies ran while one was open for 7% of the time, Pallas kernels for 0%

profile of v1, /device:TPU:6, one launch (start us, length us, event | category | flops | bytes accessed | tf_op | source)
XLA Modules:
  0.0 351.5 jit_solution(11156021777921582126)
XLA Ops:
  1.6 1.0 broadcast_in_dim.26
  2.6 7.4 %all-to-all-start = ((f32[16,51,192]{2,1,0:T(8,128)}), f32[16,51,192]{2,1,0:T(8,128)S(1)}, u32[]{:S(2)}, u32[]{:S(2)}) async-start(f32[16,51,192]{2,1,0:T(8,128)} %broadcast_in_dim.26), calls=%async_computation | async-start | bytes 1835008 | tf_op jit(solution)/shard_map/all_to_all | solution.py:34
  10.2 13.8 %all-to-all-done = f32[16,51,192]{2,1,0:T(8,128)S(1)} async-done(((f32[16,51,192]{2,1,0:T(8,128)}), f32[16,51,192]{2,1,0:T(8,128)S(1)}, u32[]{:S(2)}, u32[]{:S(2)}) %all-to-all-start) | async-done | bytes 626720 | tf_op jit(solution)/shard_map/all_to_all | solution.py:34
  24.8 1.4 slice_reduce_fusion
  26.2 1.2 slice_reduce_fusion.49
  42.0 1.4 mul.1229
  43.4 1.4 mul.1232
  52.1 15.5 %fusion.126 = (f32[2,8,8]{2,1,0:T(8,128)S(1)}, f32[2,8,8,3072]{3,2,1,0:T(8,128)S(1)}) fusion(f32[3072]{0:T(1024)} %add.442, f32[3072]{0:T(1024)} %mul.1370, f32[3072]{0:T(1024)} %mul.1367, f32[3072]{0:T(1024)} %mul.1364, f32[3072]{0:T(1024)} %mul.1361, f32[3072]{0:T(1024)} %mul.1358, f32[3072]{0:T(1024)} %mul.1355, f32[3072]{0:T(1024)} %mul.1352, ...), kind=kLoop, calls=%fused_computation.382 | loop fusion | flops 39321472 | bytes 4547072 | tf_op jit(solution)/shard_map/reduce_sum | solution.py:61
  68.6 1.6 add_reduce_fusion
  71.4 6.1 %all-to-all-start.1 = ((f32[16,2,192]{2,1,0:T(2,128)}), f32[16,2,192]{2,1,0:T(2,128)S(1)}, u32[]{:S(2)}, u32[]{:S(2)}) async-start(f32[16,2,192]{2,1,0:T(2,128)} %copy.69), calls=%async_computation.1 | async-start | bytes 65536 | tf_op jit(solution)/shard_map/all_to_all | solution.py:40
  77.6 4.7 %all-to-all-done.1 = f32[16,2,192]{2,1,0:T(2,128)S(1)} async-done(((f32[16,2,192]{2,1,0:T(2,128)}), f32[16,2,192]{2,1,0:T(2,128)S(1)}, u32[]{:S(2)}, u32[]{:S(2)}) %all-to-all-start.1) | async-done | bytes 24608 | tf_op jit(solution)/shard_map/all_to_all | solution.py:40
  83.1 6.2 %all-to-all-start.2 = ((f32[16,2,512]{2,1,0:T(2,128)}), f32[16,2,512]{2,1,0:T(2,128)S(1)}, u32[]{:S(2)}, u32[]{:S(2)}) async-start(f32[16,2,512]{2,1,0:T(2,128)} %copy.71), calls=%async_computation.2 | async-start | bytes 131072 | tf_op jit(solution)/shard_map/all_to_all | solution.py:40
  89.4 4.9 %all-to-all-done.2 = f32[16,2,512]{2,1,0:T(2,128)S(1)} async-done(((f32[16,2,512]{2,1,0:T(2,128)}), f32[16,2,512]{2,1,0:T(2,128)S(1)}, u32[]{:S(2)}, u32[]{:S(2)}) %all-to-all-start.2) | async-done | bytes 65568 | tf_op jit(solution)/shard_map/all_to_all | solution.py:40
  95.2 10.1 %all_to_all.72 = bf16[16,2,512]{2,1,0:T(2,128)(2,1)S(1)} all-to-all(bf16[16,2,512]{2,1,0:T(2,128)(2,1)S(1)} %broadcast_in_dim.27), channel_id=1, replica_groups=mesh['dp'=32,'fsdp'=16] {'fsdp'}, dimensions={0} | all-to-all | bytes 65536 | tf_op jit(solution)/shard_map/all_to_all | solution.py:34
  106.0 16.7 %all-to-all-start.4 = ((bf16[32,2,512]{2,1,0:T(2,128)(2,1)}), bf16[32,2,512]{2,1,0:T(2,128)(2,1)S(1)}, u32[]{:S(2)}, u32[]{:S(2)}) async-start(bf16[32,2,512]{2,1,0:T(2,128)(2,1)} %broadcast_in_dim.28), calls=%async_computation.4 | async-start | bytes 131072 | tf_op jit(solution)/shard_map/all_to_all | solution.py:34
  124.9 11.2 %all-to-all-done.4 = bf16[32,2,512]{2,1,0:T(2,128)(2,1)S(1)} async-done(((bf16[32,2,512]{2,1,0:T(2,128)(2,1)}), bf16[32,2,512]{2,1,0:T(2,128)(2,1)S(1)}, u32[]{:S(2)}, u32[]{:S(2)}) %all-to-all-start.4) | async-done | bytes 65568 | tf_op jit(solution)/shard_map/all_to_all | solution.py:34
  136.8 1.5 exponential_reduce_fusion.1
  138.9 6.7 %all-to-all-start.5 = ((f32[16,1,32]{2,1,0:T(1,128)}), f32[16,1,32]{2,1,0:T(1,128)}, u32[]{:S(2)}, u32[]{:S(2)}) async-start(f32[16,1,32]{2,1,0:T(1,128)} %broadcast_in_dim.29), calls=%async_computation.5 | async-start | bytes 16384 | tf_op jit(solution)/shard_map/all_to_all | solution.py:34
  146.8 3.6 %all-to-all-done.5 = f32[16,1,32]{2,1,0:T(1,128)} async-done(((f32[16,1,32]{2,1,0:T(1,128)}), f32[16,1,32]{2,1,0:T(1,128)}, u32[]{:S(2)}, u32[]{:S(2)}) %all-to-all-start.5) | async-done | bytes 2080 | tf_op jit(solution)/shard_map/all_to_all | solution.py:34
  150.4 1.3 broadcast_in_dim.30
  151.7 3.6 %all-to-all-start.6 = ((f32[32,1,64]{2,1,0:T(1,128)}), f32[32,1,64]{2,1,0:T(1,128)S(1)}, u32[]{:S(2)}, u32[]{:S(2)}) async-start(f32[32,1,64]{2,1,0:T(1,128)} %broadcast_in_dim.30), calls=%async_computation.6 | async-start | bytes 32768 | tf_op jit(solution)/shard_map/all_to_all | solution.py:34
  156.6 10.8 %all-to-all-done.6 = f32[32,1,64]{2,1,0:T(1,128)S(1)} async-done(((f32[32,1,64]{2,1,0:T(1,128)}), f32[32,1,64]{2,1,0:T(1,128)S(1)}, u32[]{:S(2)}, u32[]{:S(2)}) %all-to-all-start.6) | async-done | bytes 8224 | tf_op jit(solution)/shard_map/all_to_all | solution.py:34
  169.9 10.9 %all_to_all.73 = f32[16,2,512]{2,1,0:T(2,128)S(1)} all-to-all(f32[16,2,512]{2,1,0:T(2,128)S(1)} %copy.75), channel_id=1, replica_groups=mesh['dp'=32,'fsdp'=16] {'fsdp'}, dimensions={0} | all-to-all | bytes 131072 | tf_op jit(solution)/shard_map/all_to_all | solution.py:40
  183.7 6.2 %all-to-all-start.8 = ((bf16[16,2,512]{2,1,0:T(2,128)(2,1)}), bf16[16,2,512]{2,1,0:T(2,128)(2,1)S(1)}, u32[]{:S(2)}, u32[]{:S(2)}) async-start(bf16[16,2,512]{2,1,0:T(2,128)(2,1)} %broadcast_in_dim.31), calls=%async_computation.8 | async-start | bytes 65536 | tf_op jit(solution)/shard_map/all_to_all | solution.py:34
  189.9 1.3 broadcast_multiply_fusion.4
  191.2 3.5 all-to-all-done.8
  195.4 2.1 broadcast_multiply_fusion
  197.5 1.4 reshape.924
  198.9 6.2 %all-to-all-start.9 = ((f32[16,2,192]{2,1,0:T(2,128)}), f32[16,2,192]{2,1,0:T(2,128)S(1)}, u32[]{:S(2)}, u32[]{:S(2)}) async-start(f32[16,2,192]{2,1,0:T(2,128)} %reshape.924), calls=%async_computation.9 | async-start | bytes 65536 | tf_op jit(solution)/shard_map/all_to_all | solution.py:40
  205.1 1.3 multiply_reduce_fusion.59
  208.2 1.7 all-to-all-done.9
  214.2 1.8 multiply_reduce_fusion
  216.0 4.7 %multiply_reduce_fusion.1 = (f32[3072]{0:T(1024)}, f32[3072]{0:T(1024)}, f32[3072]{0:T(1024)}, f32[3072]{0:T(1024)}, f32[3072]{0:T(1024)}, /*index=5*/f32[3072]{...) fusion(f32[2,8,8,3072]{3,2,1,0:T(8,128)S(1)} %convert_element_t, ...), kind=kLoop, calls=%fused_computation.194 | loop fusion | flops 16066560 | bytes 4965888 | tf_op jit(solution)/shard_map/reduce_sum | solution.py:148
  220.8 3.8 %multiply_reduce_fusion.19 = (f32[3072]{0:T(1024)S(1)}, f32[3072]{0:T(1024)S(1)}, f32[3072]{0:T(1024)S(1)}, f32[3072]{0:T(1024)S(1)}, f32[3072]{0:T(1024)S(1)}, ...) fusion(f32[2,8,8,3072]{3,2,1,0:T(8,128)S(1)} %get-tuple-element, ...), kind=kLoop, calls=%fused_computation.212 | loop fusion | flops 14100480 | bytes 3366912 | tf_op jit(solution)/shard_map/reduce_sum | solution.py:148
  224.8 2.4 fusion.124
  231.8 6.1 %stack.207 = f32[52,16,192]{2,0,1:T(8,128)} concatenate(f32[1,16,192]{2,0,1:T(1,128)S(1)} %stack.156, f32[1,16,192]{2,0,1:T(1,128)S(1)} %stack.157, f32[1,16,192]{2,0,1:T(1,128)S(1)} %stack.158, f32[1,16,192]{2,0,1:T(1,128)S(1)} %stack.159, f32[1,16,192]{2,0,1:T(1,128)S(1)} %stack.160, f32[1,16,192]{2,0,1:T(1,128)S(1)} %stack.161, f32[1,16,192]{2,0,1:T(1,128)S(1)} %stack.162, ...), dimensions={0} | concatenate | bytes 1277952 | tf_op jit(solution)/shard_map/stack | solution.py:156
  237.9 6.3 %all-to-all-start.10 = ((f32[16,52,192]{2,1,0:T(8,128)}), f32[16,52,192]{2,1,0:T(8,128)S(1)}, u32[]{:S(2)}, u32[]{:S(2)}) async-start(f32[16,52,192]{2,1,0:T(8,128)} %bitcast.10), calls=%async_computation.10 | async-start | bytes 1835008 | tf_op jit(solution)/shard_map/all_to_all | solution.py:40
  244.7 13.4 %all-to-all-done.10 = f32[16,52,192]{2,1,0:T(8,128)S(1)} async-done(((f32[16,52,192]{2,1,0:T(8,128)}), f32[16,52,192]{2,1,0:T(8,128)S(1)}, u32[]{:S(2)}, u32[]{:S(2)}) %all-to-all-start.10) | async-done | bytes 639008 | tf_op jit(solution)/shard_map/all_to_all | solution.py:40
  258.4 1.1 broadcast_in_dim.34
  259.9 4.4 %all-to-all-start.11 = ((f32[32,1,3456]{2,1,0:T(1,128)}), f32[32,1,3456]{2,1,0:T(1,128)S(1)}, u32[]{:S(2)}, u32[]{:S(2)}) async-start(f32[32,1,3456]{2,1,0:T(1,128)} %broadcast_in_dim.34), calls=%async_computation.11 | async-start | bytes 884736 | tf_op jit(solution)/shard_map/all_to_all | solution.py:40
  266.1 28.2 %all-to-all-done.11 = f32[32,1,3456]{2,1,0:T(1,128)S(1)} async-done(((f32[32,1,3456]{2,1,0:T(1,128)}), f32[32,1,3456]{2,1,0:T(1,128)S(1)}, u32[]{:S(2)}, u32[]{:S(2)}) %all-to-all-start.11) | async-done | bytes 442400 | tf_op jit(solution)/shard_map/all_to_all | solution.py:40
  294.3 3.9 %all-to-all-start.13 = ((f32[32,2,512]{2,1,0:T(2,128)}), f32[32,2,512]{2,1,0:T(2,128)S(1)}, u32[]{:S(2)}, u32[]{:S(2)}) async-start(f32[32,2,512]{2,1,0:T(2,128)} %copy.80), calls=%async_computation.13 | async-start | bytes 262144 | tf_op jit(solution)/shard_map/all_to_all | solution.py:40
  298.4 15.3 %all-to-all-done.13 = f32[32,2,512]{2,1,0:T(2,128)S(1)} async-done(((f32[32,2,512]{2,1,0:T(2,128)}), f32[32,2,512]{2,1,0:T(2,128)S(1)}, u32[]{:S(2)}, u32[]{:S(2)}) %all-to-all-start.13) | async-done | bytes 131104 | tf_op jit(solution)/shard_map/all_to_all | solution.py:40
  313.7 1.0 broadcast_in_dim.35
  314.7 4.1 %all-to-all-start.12 = ((f32[32,1,3456]{2,1,0:T(1,128)}), f32[32,1,3456]{2,1,0:T(1,128)S(1)}, u32[]{:S(2)}, u32[]{:S(2)}) async-start(f32[32,1,3456]{2,1,0:T(1,128)} %broadcast_in_dim.35), calls=%async_computation.12 | async-start | bytes 884736 | tf_op jit(solution)/shard_map/all_to_all | solution.py:34
  319.3 10.6 %fusion.97 = bf16[2,8,8,3072]{3,2,1,0:T(8,128)(2,1)} fusion(f32[2,8,8,3072]{3,2,1,0:T(8,128)S(1)} %copy-done.2, f32[2,3072]{1,0:T(2,128)S(1)} %broadcast_multiply_fusion.2, f32[3072]{0:T(1024)S(1)} %copy-done.61, f32[3072]{0:T(1024)S(1)} %copy-done.60, f32[3072]{0:T(1024)S(1)} %copy-done.59, f32[3072]{0:T(1024)S(1)} %copy-done.58, f32[3072]{0:T(1024)S(1)} %copy-done.57, ...), kind=kLoop, calls=%fused_computation.248 | loop fusion | flops 38928384 | bytes 2985984 | tf_op jit(solution)/shard_map/convert_element_type | solution.py:170
  330.8 1.4 fusion.117
  332.2 14.9 %all-to-all-done.12 = f32[32,1,3456]{2,1,0:T(1,128)S(1)} async-done(((f32[32,1,3456]{2,1,0:T(1,128)}), f32[32,1,3456]{2,1,0:T(1,128)S(1)}, u32[]{:S(2)}, u32[]{:S(2)}) %all-to-all-start.12) | async-done | bytes 442400 | tf_op jit(solution)/shard_map/all_to_all | solution.py:34
  (374 shorter events, 55.6 us)
Async XLA Ops:
  0.6 81.7 %copy-start = (bf16[192,512]{1,0:T(8,128)(2,1)S(1)}, bf16[192,512]{1,0:T(8,128)(2,1)}, u32[]{:S(2)}) copy-start(bf16[192,512]{1,0:T(8,128)(2,1)} %param.12) | copy-start | bytes 589828
  2.6 21.4 %all-to-all-start = ((f32[16,51,192]{2,1,0:T(8,128)}), f32[16,51,192]{2,1,0:T(8,128)S(1)}, u32[]{:S(2)}, u32[]{:S(2)}) async-start(f32[16,51,192]{2,1,0:T(8,128)} %broadcast_in_dim.26), calls=%async_computation | async-start | bytes 1835008 | tf_op jit(solution)/shard_map/all_to_all | solution.py:34
  71.4 10.9 %all-to-all-start.1 = ((f32[16,2,192]{2,1,0:T(2,128)}), f32[16,2,192]{2,1,0:T(2,128)S(1)}, u32[]{:S(2)}, u32[]{:S(2)}) async-start(f32[16,2,192]{2,1,0:T(2,128)} %copy.69), calls=%async_computation.1 | async-start | bytes 65536 | tf_op jit(solution)/shard_map/all_to_all | solution.py:40
  83.1 11.1 %all-to-all-start.2 = ((f32[16,2,512]{2,1,0:T(2,128)}), f32[16,2,512]{2,1,0:T(2,128)S(1)}, u32[]{:S(2)}, u32[]{:S(2)}) async-start(f32[16,2,512]{2,1,0:T(2,128)} %copy.71), calls=%async_computation.2 | async-start | bytes 131072 | tf_op jit(solution)/shard_map/all_to_all | solution.py:40
  105.3 102.9 %copy-start.5 = (bf16[16,2,512]{2,1,0:T(2,128)(2,1)}, bf16[16,2,512]{2,1,0:T(2,128)(2,1)S(1)}, u32[]{:S(2)}) copy-start(bf16[16,2,512]{2,1,0:T(2,128)(2,1)S(1)} %all_to_all.72) | copy-start | bytes 98308
  106.0 30.2 %all-to-all-start.4 = ((bf16[32,2,512]{2,1,0:T(2,128)(2,1)}), bf16[32,2,512]{2,1,0:T(2,128)(2,1)S(1)}, u32[]{:S(2)}, u32[]{:S(2)}) async-start(bf16[32,2,512]{2,1,0:T(2,128)(2,1)} %broadcast_in_dim.28), calls=%async_computation.4 | async-start | bytes 131072 | tf_op jit(solution)/shard_map/all_to_all | solution.py:34
  138.9 11.5 %all-to-all-start.5 = ((f32[16,1,32]{2,1,0:T(1,128)}), f32[16,1,32]{2,1,0:T(1,128)}, u32[]{:S(2)}, u32[]{:S(2)}) async-start(f32[16,1,32]{2,1,0:T(1,128)} %broadcast_in_dim.29), calls=%async_computation.5 | async-start | bytes 16384 | tf_op jit(solution)/shard_map/all_to_all | solution.py:34
  151.7 15.8 %all-to-all-start.6 = ((f32[32,1,64]{2,1,0:T(1,128)}), f32[32,1,64]{2,1,0:T(1,128)S(1)}, u32[]{:S(2)}, u32[]{:S(2)}) async-start(f32[32,1,64]{2,1,0:T(1,128)} %broadcast_in_dim.30), calls=%async_computation.6 | async-start | bytes 32768 | tf_op jit(solution)/shard_map/all_to_all | solution.py:34
  183.7 11.0 %all-to-all-start.8 = ((bf16[16,2,512]{2,1,0:T(2,128)(2,1)}), bf16[16,2,512]{2,1,0:T(2,128)(2,1)S(1)}, u32[]{:S(2)}, u32[]{:S(2)}) async-start(bf16[16,2,512]{2,1,0:T(2,128)(2,1)} %broadcast_in_dim.31), calls=%async_computation.8 | async-start | bytes 65536 | tf_op jit(solution)/shard_map/all_to_all | solution.py:34
  198.9 11.0 %all-to-all-start.9 = ((f32[16,2,192]{2,1,0:T(2,128)}), f32[16,2,192]{2,1,0:T(2,128)S(1)}, u32[]{:S(2)}, u32[]{:S(2)}) async-start(f32[16,2,192]{2,1,0:T(2,128)} %reshape.924), calls=%async_computation.9 | async-start | bytes 65536 | tf_op jit(solution)/shard_map/all_to_all | solution.py:40
  237.9 20.3 %all-to-all-start.10 = ((f32[16,52,192]{2,1,0:T(8,128)}), f32[16,52,192]{2,1,0:T(8,128)S(1)}, u32[]{:S(2)}, u32[]{:S(2)}) async-start(f32[16,52,192]{2,1,0:T(8,128)} %bitcast.10), calls=%async_computation.10 | async-start | bytes 1835008 | tf_op jit(solution)/shard_map/all_to_all | solution.py:40
  259.5 59.4 %copy-start.16 = (f32[3072]{0:T(1024)S(1)}, f32[3072]{0:T(1024)}, u32[]{:S(2)}) copy-start(f32[3072]{0:T(1024)} %copy-done.15) | copy-start | bytes 36868
  259.5 59.4 %copy-start.18 = (f32[3072]{0:T(1024)S(1)}, f32[3072]{0:T(1024)}, u32[]{:S(2)}) copy-start(f32[3072]{0:T(1024)} %copy-done.17) | copy-start | bytes 36868
  259.5 59.4 %copy-start.20 = (f32[3072]{0:T(1024)S(1)}, f32[3072]{0:T(1024)}, u32[]{:S(2)}) copy-start(f32[3072]{0:T(1024)} %copy-done.19) | copy-start | bytes 36868
  259.6 59.4 %copy-start.22 = (f32[3072]{0:T(1024)S(1)}, f32[3072]{0:T(1024)}, u32[]{:S(2)}) copy-start(f32[3072]{0:T(1024)} %copy-done.21) | copy-start | bytes 36868
  259.6 59.4 %copy-start.24 = (f32[3072]{0:T(1024)S(1)}, f32[3072]{0:T(1024)}, u32[]{:S(2)}) copy-start(f32[3072]{0:T(1024)} %copy-done.23) | copy-start | bytes 36868
  259.6 59.4 %copy-start.26 = (f32[3072]{0:T(1024)S(1)}, f32[3072]{0:T(1024)}, u32[]{:S(2)}) copy-start(f32[3072]{0:T(1024)} %copy-done.25) | copy-start | bytes 36868
  259.6 59.4 %copy-start.28 = (f32[3072]{0:T(1024)S(1)}, f32[3072]{0:T(1024)}, u32[]{:S(2)}) copy-start(f32[3072]{0:T(1024)} %copy-done.27) | copy-start | bytes 36868
  259.6 59.4 %copy-start.30 = (f32[3072]{0:T(1024)S(1)}, f32[3072]{0:T(1024)}, u32[]{:S(2)}) copy-start(f32[3072]{0:T(1024)} %copy-done.29) | copy-start | bytes 36868
  259.6 59.4 %copy-start.32 = (f32[3072]{0:T(1024)S(1)}, f32[3072]{0:T(1024)}, u32[]{:S(2)}) copy-start(f32[3072]{0:T(1024)} %copy-done.31) | copy-start | bytes 36868
  259.6 59.4 %copy-start.34 = (f32[3072]{0:T(1024)S(1)}, f32[3072]{0:T(1024)}, u32[]{:S(2)}) copy-start(f32[3072]{0:T(1024)} %copy-done.33) | copy-start | bytes 36868
  259.6 59.4 %copy-start.36 = (f32[3072]{0:T(1024)S(1)}, f32[3072]{0:T(1024)}, u32[]{:S(2)}) copy-start(f32[3072]{0:T(1024)} %copy-done.35) | copy-start | bytes 36868
  259.6 59.4 %copy-start.38 = (f32[3072]{0:T(1024)S(1)}, f32[3072]{0:T(1024)}, u32[]{:S(2)}) copy-start(f32[3072]{0:T(1024)} %copy-done.37) | copy-start | bytes 36868
  259.6 59.4 %copy-start.40 = (f32[3072]{0:T(1024)S(1)}, f32[3072]{0:T(1024)}, u32[]{:S(2)}) copy-start(f32[3072]{0:T(1024)} %copy-done.39) | copy-start | bytes 36868
  259.7 59.4 %copy-start.42 = (f32[3072]{0:T(1024)S(1)}, f32[3072]{0:T(1024)}, u32[]{:S(2)}) copy-start(f32[3072]{0:T(1024)} %copy-done.41) | copy-start | bytes 36868
  259.7 59.4 %copy-start.43 = (f32[3072]{0:T(1024)S(1)}, f32[3072]{0:T(1024)}, u32[]{:S(2)}) copy-start(f32[3072]{0:T(1024)} %mul.1316) | copy-start | bytes 36868
  259.7 59.4 %copy-start.44 = (f32[3072]{0:T(1024)S(1)}, f32[3072]{0:T(1024)}, u32[]{:S(2)}) copy-start(f32[3072]{0:T(1024)} %mul.1319) | copy-start | bytes 36868
  259.7 59.4 %copy-start.45 = (f32[3072]{0:T(1024)S(1)}, f32[3072]{0:T(1024)}, u32[]{:S(2)}) copy-start(f32[3072]{0:T(1024)} %mul.1322) | copy-start | bytes 36868
  259.7 59.4 %copy-start.46 = (f32[3072]{0:T(1024)S(1)}, f32[3072]{0:T(1024)}, u32[]{:S(2)}) copy-start(f32[3072]{0:T(1024)} %mul.1325) | copy-start | bytes 36868
  259.7 59.4 %copy-start.47 = (f32[3072]{0:T(1024)S(1)}, f32[3072]{0:T(1024)}, u32[]{:S(2)}) copy-start(f32[3072]{0:T(1024)} %mul.1328) | copy-start | bytes 36868
  259.7 59.4 %copy-start.48 = (f32[3072]{0:T(1024)S(1)}, f32[3072]{0:T(1024)}, u32[]{:S(2)}) copy-start(f32[3072]{0:T(1024)} %mul.1331) | copy-start | bytes 36868
  259.7 59.4 %copy-start.49 = (f32[3072]{0:T(1024)S(1)}, f32[3072]{0:T(1024)}, u32[]{:S(2)}) copy-start(f32[3072]{0:T(1024)} %mul.1334) | copy-start | bytes 36868
  259.7 59.4 %copy-start.50 = (f32[3072]{0:T(1024)S(1)}, f32[3072]{0:T(1024)}, u32[]{:S(2)}) copy-start(f32[3072]{0:T(1024)} %mul.1337) | copy-start | bytes 36868
  259.7 59.4 %copy-start.51 = (f32[3072]{0:T(1024)S(1)}, f32[3072]{0:T(1024)}, u32[]{:S(2)}) copy-start(f32[3072]{0:T(1024)} %mul.1340) | copy-start | bytes 36868
  259.8 59.4 %copy-start.52 = (f32[3072]{0:T(1024)S(1)}, f32[3072]{0:T(1024)}, u32[]{:S(2)}) copy-start(f32[3072]{0:T(1024)} %mul.1343) | copy-start | bytes 36868
  259.8 59.4 %copy-start.53 = (f32[3072]{0:T(1024)S(1)}, f32[3072]{0:T(1024)}, u32[]{:S(2)}) copy-start(f32[3072]{0:T(1024)} %mul.1346) | copy-start | bytes 36868
  259.8 59.4 %copy-start.54 = (f32[3072]{0:T(1024)S(1)}, f32[3072]{0:T(1024)}, u32[]{:S(2)}) copy-start(f32[3072]{0:T(1024)} %mul.1349) | copy-start | bytes 36868
  259.8 59.4 %copy-start.55 = (f32[3072]{0:T(1024)S(1)}, f32[3072]{0:T(1024)}, u32[]{:S(2)}) copy-start(f32[3072]{0:T(1024)} %mul.1352) | copy-start | bytes 36868
  259.8 59.4 %copy-start.56 = (f32[3072]{0:T(1024)S(1)}, f32[3072]{0:T(1024)}, u32[]{:S(2)}) copy-start(f32[3072]{0:T(1024)} %mul.1355) | copy-start | bytes 36868
  259.8 59.4 %copy-start.57 = (f32[3072]{0:T(1024)S(1)}, f32[3072]{0:T(1024)}, u32[]{:S(2)}) copy-start(f32[3072]{0:T(1024)} %mul.1358) | copy-start | bytes 36868
  259.8 59.4 %copy-start.58 = (f32[3072]{0:T(1024)S(1)}, f32[3072]{0:T(1024)}, u32[]{:S(2)}) copy-start(f32[3072]{0:T(1024)} %mul.1361) | copy-start | bytes 36868
  259.8 59.4 %copy-start.59 = (f32[3072]{0:T(1024)S(1)}, f32[3072]{0:T(1024)}, u32[]{:S(2)}) copy-start(f32[3072]{0:T(1024)} %mul.1364) | copy-start | bytes 36868
  259.8 59.4 %copy-start.60 = (f32[3072]{0:T(1024)S(1)}, f32[3072]{0:T(1024)}, u32[]{:S(2)}) copy-start(f32[3072]{0:T(1024)} %mul.1367) | copy-start | bytes 36868
  259.8 59.4 %copy-start.61 = (f32[3072]{0:T(1024)S(1)}, f32[3072]{0:T(1024)}, u32[]{:S(2)}) copy-start(f32[3072]{0:T(1024)} %mul.1370) | copy-start | bytes 36868
  259.9 59.4 %copy-start.62 = (f32[3072]{0:T(1024)S(1)}, f32[3072]{0:T(1024)}, u32[]{:S(2)}) copy-start(f32[3072]{0:T(1024)} %mul.1229) | copy-start | bytes 36868
  259.9 34.4 %all-to-all-start.11 = ((f32[32,1,3456]{2,1,0:T(1,128)}), f32[32,1,3456]{2,1,0:T(1,128)S(1)}, u32[]{:S(2)}, u32[]{:S(2)}) async-start(f32[32,1,3456]{2,1,0:T(1,128)} %broadcast_in_dim.34), calls=%async_computation.11 | async-start | bytes 884736 | tf_op jit(solution)/shard_map/all_to_all | solution.py:40
  294.3 19.4 %all-to-all-start.13 = ((f32[32,2,512]{2,1,0:T(2,128)}), f32[32,2,512]{2,1,0:T(2,128)S(1)}, u32[]{:S(2)}, u32[]{:S(2)}) async-start(f32[32,2,512]{2,1,0:T(2,128)} %copy.80), calls=%async_computation.13 | async-start | bytes 262144 | tf_op jit(solution)/shard_map/all_to_all | solution.py:40
  314.7 32.3 %all-to-all-start.12 = ((f32[32,1,3456]{2,1,0:T(1,128)}), f32[32,1,3456]{2,1,0:T(1,128)S(1)}, u32[]{:S(2)}, u32[]{:S(2)}) async-start(f32[32,1,3456]{2,1,0:T(1,128)} %broadcast_in_dim.35), calls=%async_computation.12 | async-start | bytes 884736 | tf_op jit(solution)/shard_map/all_to_all | solution.py:34
  (61 other events, 1284.6 us)

commit v2 on v0

v2 whole, which is shorter than its diff:
```python
import jax
import jax.numpy as jnp
from jax import lax
from jax.experimental import pallas as pl
from jax.experimental.pallas import tpu as pltpu
from jax.sharding import PartitionSpec as P

KERNEL = 7
MAP_SIDE = 8
LOGIT_SCALE = 14.0
EPSILON = 1e-06
MESH = pl.DeviceIdType.MESH
F32 = jnp.float32
BF16 = jnp.bfloat16
N_DP = 32
N_FSDP = 16
IMGS = 2
CHANNELS = 3072
SHARD = 192
EMBED = 512
ROWS = 56
BIAS_ROW, BLOCK_ROW, HEAD_ROW, LOSS_ROW = 49, 50, 51, 52
BLOCKS = CHANNELS // 128
VMEM_SPEC = pl.BlockSpec(memory_space=pltpu.VMEM)


def contract(left, right, left_dim, right_dim):
    return lax.dot_general(
        left, right, (((left_dim,), (right_dim,)), ((), ())), preferred_element_type=F32
    )


def copy_to(axis, peer, src, dst, send_sem, recv_sem):
    return pltpu.make_async_remote_copy(
        src_ref=src,
        dst_ref=dst,
        send_sem=send_sem,
        recv_sem=recv_sem,
        device_id={axis: peer},
        device_id_type=MESH,
    )


def loop(low, high, body):
    def step(t, carry):
        body(t)
        return carry

    lax.fori_loop(low, high, step, 0)


def greet(me_f, me_d, with_dp):
    barrier = pltpu.get_barrier_semaphore()

    def signal(axis, me, count):
        def body(t):
            peer = lax.rem(me + t, count)
            pl.semaphore_signal(barrier, inc=1, device_id={axis: peer}, device_id_type=MESH)

        loop(1, count, body)

    total = N_FSDP - 1
    if with_dp:
        signal("dp", me_d, N_DP)
        total += N_DP - 1
    signal("fsdp", me_f, N_FSDP)
    pl.semaphore_wait(barrier, total)


class Exchange:
    def __init__(self, axis, count, me, source, dst, send_sem, recv_sem):
        self.axis, self.count, self.me = axis, count, me
        self.source, self.dst, self.send_sem, self.recv_sem = source, dst, send_sem, recv_sem

    def _each(self, act):
        def body(t):
            act(t, lax.rem(self.me + t, self.count))

        loop(1, self.count, body)

    def start(self):
        def act(t, peer):
            copy_to(
                self.axis, peer, self.source(peer), self.dst.at[self.me],
                self.send_sem.at[t], self.recv_sem.at[self.me],
            ).start()

        self._each(act)

    def wait_recv(self):
        def act(t, peer):
            copy_to(
                self.axis, peer, self.source(peer), self.dst.at[peer],
                self.send_sem.at[t], self.recv_sem.at[peer],
            ).wait_recv()

        self._each(act)

    def wait_send(self):
        def act(t, peer):
            copy_to(
                self.axis, peer, self.source(peer), self.dst.at[self.me],
                self.send_sem.at[t], self.recv_sem.at[self.me],
            ).wait_send()

        self._each(act)


def join_pairs(read, write):
    for p in range(N_FSDP // 2):
        write(p, jnp.concatenate([read(2 * p), read(2 * p + 1)], axis=1))


def shifted(value, amount):
    if amount == 0:
        return value
    place = lax.broadcasted_iota(jnp.int32, value.shape, 0)
    rolled = pltpu.roll(value, amount % MAP_SIDE, 0)
    inside = place >= amount if amount > 0 else place < MAP_SIDE + amount
    return jnp.where(inside, rolled, 0.0)


def lanes_of(block):
    return pl.ds(pl.multiple_of(block * 128, 128), 128)


def gather_kernel(w_ref, bias_ref, gain_ref, full_ref, pack, held, send_sem, recv_sem):
    me_f, me_d = lax.axis_index("fsdp"), lax.axis_index("dp")
    rows = jnp.concatenate(
        [w_ref[...], bias_ref[...], gain_ref[...], jnp.zeros((ROWS - 51, SHARD), F32)], axis=0
    )
    pack[...] = rows
    held[me_f] = rows
    greet(me_f, me_d, False)
    ex = Exchange("fsdp", N_FSDP, me_f, lambda peer: pack, held, send_sem, recv_sem)
    ex.start()
    ex.wait_recv()

    def write(p, value):
        full_ref[:, 384 * p : 384 * (p + 1)] = value

    join_pairs(lambda s: held[s], write)
    ex.wait_send()


def forward_kernel(images, full, z_ref, inv_ref, zsum_ref, normed_ref, poolinv_ref, sums, isum, pooled):
    margin = KERNEL // 2
    sums[...] = jnp.zeros_like(sums)

    def conv(block):
        lanes = lanes_of(block)
        for b in range(IMGS):
            rows = [images[b, i, :, lanes].astype(F32) for i in range(MAP_SIDE)]
            total = rows[0]
            for i in range(1, MAP_SIDE):
                total = total + rows[i]
            isum[b, :, lanes] = total
            bias = jnp.broadcast_to(full[pl.ds(BIAS_ROW, 1), lanes], (MAP_SIDE, 128))
            acc = [bias] * MAP_SIDE
            for s in range(KERNEL):
                cols = [shifted(row, margin - s) for row in rows]
                for r in range(KERNEL):
                    tap = jnp.broadcast_to(
                        full[pl.ds(r * KERNEL + s, 1), lanes], (MAP_SIDE, 128)
                    )
                    for i in range(MAP_SIDE):
                        if 0 <= i + r - margin < MAP_SIDE:
                            acc[i] = acc[i] + cols[i + r - margin] * tap
            for i in range(MAP_SIDE):
                z_ref[b, i, :, lanes] = acc[i]
                sums[b, i] += acc[i]

    loop(0, BLOCKS, conv)
    mean = jnp.sum(sums[...], axis=3, keepdims=True) * (1.0 / CHANNELS)
    mean = jnp.broadcast_to(mean, sums.shape)
    inv_ref[...] = mean
    sums[...] = jnp.zeros_like(sums)

    def centre(block):
        lanes = lanes_of(block)
        value = z_ref[:, :, :, lanes] - inv_ref[...]
        z_ref[:, :, :, lanes] = value
        sums[...] += value * value

    loop(0, BLOCKS, centre)
    var = jnp.sum(sums[...], axis=3, keepdims=True) * (1.0 / CHANNELS)
    inv_ref[...] = jnp.broadcast_to(lax.rsqrt(var + EPSILON), sums.shape)

    def norm(block):
        lanes = lanes_of(block)
        value = z_ref[:, :, :, lanes] * inv_ref[...]
        z_ref[:, :, :, lanes] = value
        zs = jnp.sum(jnp.sum(value, axis=1), axis=1)
        zsum_ref[:, lanes] = zs
        gain = full[pl.ds(BLOCK_ROW, 1), lanes]
        img = jnp.sum(isum[:, :, lanes], axis=1)
        pooled[:, lanes] = (img + zs * gain) * (1.0 / (MAP_SIDE * MAP_SIDE))

    loop(0, BLOCKS, norm)
    value = pooled[...]
    centred = value - jnp.mean(value, axis=1, keepdims=True)
    inverse = lax.rsqrt(jnp.mean(centred * centred, axis=1, keepdims=True) + EPSILON)
    poolinv_ref[...] = jnp.broadcast_to(inverse, poolinv_ref.shape)
    normed_ref[...] = centred * inverse


def loss_kernel(
    normed_ref, head_ref, proj_ref, text_ref,
    dnormed_ref, projgrad_ref, headgrad_ref, losspart_ref, gtext_ref,
    normed_s, normed_r, part_s, part_r, img_s, img_r, row_s, row_r, dimg_s, dimg_r,
    demb_s, demb_r, dn_s, dn_r, text_s, text_r, col_s, col_r, dcap_s, dcap_r,
    fs, fr, ds, dr,
):
    me_f, me_d = lax.axis_index("fsdp"), lax.axis_index("dp")

    def fex(n, source, dst):
        return Exchange("fsdp", N_FSDP, me_f, source, dst, fs.at[n], fr.at[n])

    def dex(n, source, dst):
        return Exchange("dp", N_DP, me_d, source, dst, ds.at[n], dr.at[n])

    def stack(ref, count):
        return jnp.concatenate([ref[k] for k in range(count)], axis=0)

    def total(ref, count):
        out = ref[0]
        for k in range(1, count):
            out = out + ref[k]
        return out

    def spread(ref, value):
        for k in range(ref.shape[0]):
            ref[k] = value[IMGS * k : IMGS * (k + 1)]

    text = text_ref[...].astype(F32)
    text_scale = lax.rsqrt(jnp.sum(text * text, axis=1, keepdims=True) + EPSILON)
    text_f = text * text_scale
    text_unit = text_f.astype(BF16)
    text_s[...] = text_unit
    text_r[me_d] = text_unit
    for p in range(N_FSDP // 2):
        value = normed_ref[:, 384 * p : 384 * (p + 1)]
        normed_s[2 * p] = value[:, :SHARD]
        normed_s[2 * p + 1] = value[:, SHARD:]
    normed_r[me_f] = normed_s[me_f]
    greet(me_f, me_d, True)
    x_norm = fex(0, lambda peer: normed_s.at[peer], normed_r)
    x_norm.start()
    x_text = dex(0, lambda peer: text_s, text_r)
    x_text.start()
    x_norm.wait_recv()
    normed = stack(normed_r, N_FSDP)
    head = head_ref[...]
    query = (normed * head).astype(BF16)
    part = jnp.dot(query, proj_ref[...], preferred_element_type=F32)
    spread(part_s, part)
    part_r[me_f] = part_s[me_f]
    x_part = fex(1, lambda peer: part_s.at[peer], part_r)
    x_part.start()
    x_part.wait_recv()
    embedding = total(part_r, N_FSDP)
    image_scale = lax.rsqrt(jnp.sum(embedding * embedding, axis=1, keepdims=True) + EPSILON)
    image_f = embedding * image_scale
    image_unit = image_f.astype(BF16)
    img_s[...] = image_unit
    img_r[me_f] = image_unit
    x_img = fex(2, lambda peer: img_s, img_r)
    x_img.start()
    diagonal = LOGIT_SCALE * jnp.sum(image_unit.astype(F32) * text_unit.astype(F32))
    x_text.wait_recv()
    text_cols = stack(text_r, N_DP)
    x_img.wait_recv()
    image_rows = stack(img_r, N_FSDP)
    n_row, n_col = N_FSDP * IMGS, N_DP * IMGS
    logits = LOGIT_SCALE * contract(image_rows, text_cols, 1, 1)
    exps = jnp.exp(logits)
    col_part = jnp.sum(exps, axis=0, keepdims=True)
    row_part = jnp.sum(exps, axis=1, keepdims=True)
    eye = (
        lax.broadcasted_iota(jnp.int32, (n_row, 128), 0)
        == lax.broadcasted_iota(jnp.int32, (n_row, 128), 1)
    )
    row_flat = jnp.sum(jnp.where(eye, row_part, 0.0), axis=0, keepdims=True)
    col_flat = jnp.concatenate([col_part, jnp.zeros((1, 128 - n_col), F32)], axis=1)
    col_s[...] = col_flat
    col_r[me_d] = col_flat
    x_col = dex(1, lambda peer: col_s, col_r)
    x_col.start()
    row_s[...] = row_flat
    row_r[me_f] = row_flat
    x_row = fex(3, lambda peer: row_s, row_r)
    x_row.start()
    x_row.wait_recv()
    row_sum = total(row_r, N_FSDP)
    row_lse = jnp.log(jnp.sum(jnp.where(eye, row_sum, 0.0), axis=1, keepdims=True))
    row_term = jnp.exp(logits - row_lse)
    at_row = lax.broadcasted_iota(jnp.int32, (n_row, n_col), 0)
    at_col = lax.broadcasted_iota(jnp.int32, (n_row, n_col), 1)
    pair = jnp.where(
        (at_row - IMGS * me_f == at_col - IMGS * me_d)
        & (at_row >= IMGS * me_f)
        & (at_row < IMGS * me_f + IMGS),
        2.0,
        0.0,
    )
    x_col.wait_recv()
    col_lse = jnp.log(total(col_r, N_DP)[:, :n_col])
    weights = (row_term + jnp.exp(logits - col_lse) - pair).astype(BF16)
    dimg = jnp.dot(weights, text_cols, preferred_element_type=F32)
    spread(dimg_s, dimg)
    dimg_r[me_f] = dimg_s[me_f]
    x_dimg = fex(4, lambda peer: dimg_s.at[peer], dimg_r)
    x_dimg.start()
    dcap = contract(weights, image_rows, 0, 0)
    spread(dcap_s, dcap)
    dcap_r[me_d] = dcap_s[me_d]
    x_dcap = dex(2, lambda peer: dcap_s.at[peer], dcap_r)
    x_dcap.start()
    loss_part = (
        jnp.sum(row_lse) * (1.0 / N_FSDP) + jnp.sum(col_lse) * (1.0 / N_DP) - 2.0 * diagonal
    )
    losspart_ref[...] = jnp.full(losspart_ref.shape, loss_part, F32)
    x_dimg.wait_recv()
    d_image = 7.0 * total(dimg_r, N_FSDP)
    d_embedding = (
        image_scale * (d_image - image_f * jnp.sum(image_f * d_image, axis=1, keepdims=True))
    ).astype(BF16)
    demb_s[...] = d_embedding
    demb_r[me_f] = d_embedding
    x_demb = fex(5, lambda peer: demb_s, demb_r)
    x_demb.start()
    x_demb.wait_recv()
    demb = stack(demb_r, N_FSDP)
    d_query = contract(demb, proj_ref[...], 1, 1)
    spread(dn_s, d_query * head)
    dn_r[me_f] = dn_s[me_f]
    x_dn = fex(6, lambda peer: dn_s.at[peer], dn_r)
    x_dn.start()
    headgrad_ref[...] = jnp.sum(d_query * normed, axis=0, keepdims=True)
    projgrad_ref[...] = contract(query, demb, 0, 0)
    x_dcap.wait_recv()
    d_caption = 7.0 * total(dcap_r, N_DP)
    gtext_ref[...] = text_scale * (
        d_caption - text_f * jnp.sum(text_f * d_caption, axis=1, keepdims=True)
    )
    x_dn.wait_recv()

    def write(p, value):
        dnormed_ref[:, 384 * p : 384 * (p + 1)] = value

    join_pairs(lambda k: dn_r[k], write)
    for ex in (x_norm, x_text, x_part, x_img, x_col, x_row, x_dimg, x_dcap, x_demb, x_dn):
        ex.wait_send()


def backward_kernel(
    images, z_ref, inv_ref, full, zsum_ref, dnormed_ref, normed_ref, poolinv_ref, losspart_ref,
    gimg_ref, blocks_ref,
    grads, dh, dn, sums, mean1,
):
    margin = KERNEL // 2
    normed = normed_ref[...]
    d_normed = dnormed_ref[...]
    d_pooled = poolinv_ref[:, :1] * (
        d_normed
        - jnp.mean(d_normed, axis=1, keepdims=True)
        - normed * jnp.mean(d_normed * normed, axis=1, keepdims=True)
    )
    d_hidden = d_pooled * (1.0 / (MAP_SIDE * MAP_SIDE))
    dh[...] = d_hidden
    d_norm = d_hidden * full[BLOCK_ROW : BLOCK_ROW + 1, :]
    dn[...] = d_norm
    grads[ROWS - 8 :, :] = jnp.zeros((8, CHANNELS), F32)
    grads[BLOCK_ROW : BLOCK_ROW + 1, :] = jnp.sum(d_hidden * zsum_ref[...], axis=0, keepdims=True)
    grads[LOSS_ROW : LOSS_ROW + 1, :] = jnp.broadcast_to(losspart_ref[:, :1], (1, CHANNELS))
    mean1[...] = jnp.broadcast_to(jnp.mean(d_norm, axis=1, keepdims=True), mean1.shape)
    sums[...] = jnp.zeros_like(sums)

    def project(block):
        lanes = lanes_of(block)
        for b in range(IMGS):
            row = jnp.broadcast_to(dn[pl.ds(b, 1), lanes], (MAP_SIDE, 128))
            for i in range(MAP_SIDE):
                sums[b, i] += row * z_ref[b, i, :, lanes]

    loop(0, BLOCKS, project)
    mean2 = jnp.sum(sums[...], axis=3, keepdims=True) * (1.0 / CHANNELS)
    sums[...] = jnp.broadcast_to(mean2, sums.shape)

    def conv(block):
        lanes = lanes_of(block)
        maps, pixels, acc = [], [], []
        bias = None
        for b in range(IMGS):
            row = jnp.broadcast_to(dn[pl.ds(b, 1), lanes], (MAP_SIDE, 128)) - jnp.broadcast_to(
                mean1[pl.ds(b, 1), :], (MAP_SIDE, 128)
            )
            hidden = jnp.broadcast_to(dh[pl.ds(b, 1), lanes], (MAP_SIDE, 128))
            for i in range(MAP_SIDE):
                value = inv_ref[b, i] * (row - z_ref[b, i, :, lanes] * sums[b, i])
                maps.append(value)
                bias = value if bias is None else bias + value
                pixels.append(images[b, i, :, lanes].astype(F32))
                acc.append(hidden)
        grads[pl.ds(BIAS_ROW, 1), lanes] = jnp.sum(bias, axis=0, keepdims=True)
        for s in range(KERNEL):
            cols = [shifted(value, s - margin) for value in maps]
            for r in range(KERNEL):
                tap = jnp.broadcast_to(full[pl.ds(r * KERNEL + s, 1), lanes], (MAP_SIDE, 128))
                grad = None
                for b in range(IMGS):
                    for i in range(MAP_SIDE):
                        if 0 <= i - r + margin < MAP_SIDE:
                            col = cols[b * MAP_SIDE + i - r + margin]
                            k = b * MAP_SIDE + i
                            acc[k] = acc[k] + col * tap
                            term = col * pixels[k]
                            grad = term if grad is None else grad + term
                grads[pl.ds(r * KERNEL + s, 1), lanes] = jnp.sum(grad, axis=0, keepdims=True)
        for b in range(IMGS):
            for i in range(MAP_SIDE):
                gimg_ref[b, i, :, lanes] = acc[b * MAP_SIDE + i].astype(BF16)

    loop(0, BLOCKS, conv)
    for p in range(N_FSDP // 2):
        value = grads[:, 384 * p : 384 * (p + 1)]
        blocks_ref[2 * p] = value[:, :SHARD]
        blocks_ref[2 * p + 1] = value[:, SHARD:]


PROJ_OWNERS = SHARD // 8
SMALL_OWNERS = ROWS // 8


def reduce_kernel(
    blocks_ref, headgrad_ref, projgrad_ref, small_ref, proj_ref,
    held_r, small, proj_r, small_r, proj_mine, small_mine, proj_all, small_all,
    fs, fr, ps, pr, ss, sr, gs, gr,
):
    me_f, me_d = lax.axis_index("fsdp"), lax.axis_index("dp")
    held_r[me_f] = blocks_ref[me_f]
    greet(me_f, me_d, True)
    first = PROJ_OWNERS
    last = PROJ_OWNERS + SMALL_OWNERS

    def proj_rows(k):
        return pl.ds(pl.multiple_of(k * 8, 8), 8)

    def small_rows(k):
        return pl.ds(pl.multiple_of((k - first) * 8, 8), 8)

    def peers(act):
        def body(t):
            act(t, lax.rem(me_d + t, N_DP))

        loop(1, N_DP, body)

    def proj_copy(t, peer, to):
        return copy_to("dp", peer, projgrad_ref.at[proj_rows(to)], proj_r.at[me_d], ps.at[t], pr.at[me_d])

    def small_copy(t, peer, to):
        return copy_to("dp", peer, small.at[small_rows(to)], small_r.at[me_d], ss.at[t], sr.at[me_d])

    def start_proj(t, peer):
        @pl.when(peer < first)
        def _():
            proj_copy(t, peer, peer).start()

    peers(start_proj)
    ex = Exchange("fsdp", N_FSDP, me_f, lambda peer: blocks_ref.at[peer], held_r, fs, fr)
    ex.start()
    ex.wait_recv()
    held = held_r[0]
    for k in range(1, N_FSDP):
        held = held + held_r[k]
    small[...] = held
    small[HEAD_ROW : HEAD_ROW + 1, :] = headgrad_ref[...]

    def start_small(t, peer):
        @pl.when((peer >= first) & (peer < last))
        def _():
            small_copy(t, peer, peer).start()

    peers(start_small)

    def all_copy(t, peer, sender, mine, everyone, slot):
        return copy_to("dp", peer, mine, everyone.at[slot], gs.at[t], gr.at[sender])

    @pl.when(me_d < first)
    def _():
        proj_r[me_d] = projgrad_ref[proj_rows(me_d), :]

        def wait(t, peer):
            copy_to(
                "dp", peer, projgrad_ref.at[proj_rows(0)], proj_r.at[peer], ps.at[t], pr.at[peer]
            ).wait_recv()

        peers(wait)
        out = proj_r[0]
        for k in range(1, N_DP):
            out = out + proj_r[k]
        proj_mine[...] = out
        proj_all[me_d] = out
        peers(lambda t, peer: all_copy(t, peer, me_d, proj_mine, proj_all, me_d).start())

    @pl.when((me_d >= first) & (me_d < last))
    def _():
        small_r[me_d] = small[small_rows(me_d), :]

        def wait(t, peer):
            copy_to(
                "dp", peer, small.at[small_rows(first)], small_r.at[peer], ss.at[t], sr.at[peer]
            ).wait_recv()

        peers(wait)
        out = small_r[0]
        for k in range(1, N_DP):
            out = out + small_r[k]
        small_mine[...] = out
        small_all[me_d - first] = out
        peers(lambda t, peer: all_copy(t, peer, me_d, small_mine, small_all, me_d - first).start())

    def wait_all(t, peer):
        @pl.when(peer < first)
        def _():
            all_copy(t, peer, peer, proj_mine, proj_all, peer).wait_recv()

        @pl.when((peer >= first) & (peer < last))
        def _():
            all_copy(t, peer, peer, small_mine, small_all, peer - first).wait_recv()

    peers(wait_all)
    for k in range(PROJ_OWNERS):
        proj_ref[8 * k : 8 * (k + 1), :] = proj_all[k]
    for k in range(SMALL_OWNERS):
        small_ref[8 * k : 8 * (k + 1), :] = small_all[k]
    ex.wait_send()

    def drain(t, peer):
        @pl.when(peer < first)
        def _():
            proj_copy(t, peer, peer).wait_send()

        @pl.when((peer >= first) & (peer < last))
        def _():
            small_copy(t, peer, peer).wait_send()

        @pl.when(me_d < first)
        def _():
            all_copy(t, peer, me_d, proj_mine, proj_all, me_d).wait_send()

        @pl.when((me_d >= first) & (me_d < last))
        def _():
            all_copy(t, peer, me_d, small_mine, small_all, me_d - first).wait_send()

    peers(drain)


def call(kernel, inputs, outs, scratch, collective=None):
    params = dict(vmem_limit_bytes=48 * 1024 * 1024)
    if collective is not None:
        params.update(collective_id=collective, has_side_effects=True)
    return pl.pallas_call(
        kernel,
        out_shape=[jax.ShapeDtypeStruct(s, d) for s, d in outs],
        in_specs=[VMEM_SPEC] * len(inputs),
        out_specs=[VMEM_SPEC] * len(outs),
        scratch_shapes=scratch,
        compiler_params=pltpu.CompilerParams(**params),
    )(*inputs)


def dma(*shape):
    return pltpu.SemaphoreType.DMA(shape)


def local(images, dw_weight, dw_bias, block_gain, head_gain, projection, text):
    V = pltpu.VMEM
    maps = (IMGS, MAP_SIDE, MAP_SIDE, CHANNELS)
    lanes = (IMGS, MAP_SIDE, MAP_SIDE, 128)
    wide = (IMGS, CHANNELS)
    (full,) = call(
        gather_kernel,
        (dw_weight, dw_bias[None], block_gain[None]),
        [((ROWS, CHANNELS), F32)],
        [V((ROWS, SHARD), F32), V((N_FSDP, ROWS, SHARD), F32), dma(N_FSDP), dma(N_FSDP)],
        0,
    )
    z, inv, zsum, normed, poolinv = call(
        forward_kernel,
        (images, full),
        [(maps, F32), (lanes, F32), (wide, F32), (wide, F32), ((IMGS, 128), F32)],
        [V(lanes, F32), V((IMGS, MAP_SIDE, CHANNELS), F32), V(wide, F32)],
    )
    two = (IMGS, EMBED)
    f_blocks = lambda shape, kind: V((N_FSDP,) + shape, kind)
    d_blocks = lambda shape, kind: V((N_DP,) + shape, kind)
    dnormed, projgrad, headgrad, losspart, grad_text = call(
        loss_kernel,
        (normed, head_gain[None], projection, text),
        [(wide, F32), ((SHARD, EMBED), F32), ((1, SHARD), F32), ((1, 128), F32), (two, F32)],
        [
            f_blocks((IMGS, SHARD), F32), f_blocks((IMGS, SHARD), F32),
            f_blocks(two, F32), f_blocks(two, F32),
            V(two, BF16), f_blocks(two, BF16),
            V((1, 128), F32), f_blocks((1, 128), F32),
            f_blocks(two, F32), f_blocks(two, F32),
            V(two, BF16), f_blocks(two, BF16),
            f_blocks((IMGS, SHARD), F32), f_blocks((IMGS, SHARD), F32),
            V(two, BF16), d_blocks(two, BF16),
            V((1, 128), F32), d_blocks((1, 128), F32),
            d_blocks(two, F32), d_blocks(two, F32),
            dma(7, N_FSDP), dma(7, N_FSDP), dma(3, N_DP), dma(3, N_DP),
        ],
        1,
    )
    grad_images, blocks = call(
        backward_kernel,
        (images, z, inv, full, zsum, dnormed, normed, poolinv, losspart),
        [(maps, BF16), ((N_FSDP, ROWS, SHARD), F32)],
        [V((ROWS, CHANNELS), F32), V(wide, F32), V(wide, F32), V(lanes, F32), V((IMGS, 128), F32)],
    )
    sums, sum_proj = call(
        reduce_kernel,
        (blocks, headgrad, projgrad),
        [((ROWS, SHARD), F32), ((SHARD, EMBED), F32)],
        [
            f_blocks((ROWS, SHARD), F32), V((ROWS, SHARD), F32),
            d_blocks((8, EMBED), F32), d_blocks((8, SHARD), F32),
            V((8, EMBED), F32), V((8, SHARD), F32),
            V((PROJ_OWNERS, 8, EMBED), F32), V((SMALL_OWNERS, 8, SHARD), F32),
            dma(N_FSDP), dma(N_FSDP), dma(N_DP), dma(N_DP), dma(N_DP), dma(N_DP), dma(N_DP), dma(N_DP),
        ],
        2,
    )
    return (
        sums[LOSS_ROW, 0] / (2.0 * N_DP * N_FSDP * IMGS),
        grad_images,
        sums[: KERNEL * KERNEL],
        sums[BIAS_ROW],
        sums[BLOCK_ROW],
        sums[HEAD_ROW],
        sum_proj,
        grad_text,
    )


def solution(mesh):
    return jax.shard_map(
        local,
        mesh=mesh,
        in_specs=(
            P(("dp", "fsdp"), None, None, None),
            P(None, "fsdp"),
            P("fsdp"),
            P("fsdp"),
            P("fsdp"),
            P("fsdp", None),
            P(("dp", "fsdp"), None),
        ),
        out_specs=(
            P(),
            P(("dp", "fsdp"), None, None, None),
            P(None, "fsdp"),
            P("fsdp"),
            P("fsdp"),
            P("fsdp"),
            P("fsdp", None),
            P(("dp", "fsdp"), None),
        ),
        check_vma=False,
    )
```

time: 2230 us -> 166 us (0.07)
  waiting for transfers between devices: 1730 us -> 0 us
  blocking collectives: 393 us -> 0 us
  Pallas kernels: 0 us -> 156 us
  other arithmetic: 47 us -> 0 us
    all_gather x3 -> x0, waiting for transfers between devices: 1510 us -> none  [the longest x1 756 us: local(): lax.all_gather(text_unit, ('dp', 'fsdp'), axis=0, tiled=True)]
    unnamed x3 -> x0, blocking collectives: 229 us -> none
    pallas_call x0 -> x5, Pallas kernels: none -> 156 us  [call(): pl.pallas_call(kernel, out_shape=[jax.ShapeDtypeStruct(s, d) for s, d in...]
    psum x1 -> x0, waiting for transfers between devices: 145 us -> none  [local(): lax.psum((part_weight, part_bias, part_block, part_head, proj_grad), 'dp')]
    psum x1 -> x0, blocking collectives: 119 us -> none  [local(): lax.psum((part_weight, part_bias, part_block, part_head, proj_grad), 'dp')]
    unnamed x6 -> x0, waiting for transfers between devices: 72.2 us -> none
    all_gather x2 -> x0, blocking collectives: 44.6 us -> none  [the longest x1 24.1 us: local(): lax.all_gather(dw_weight, 'fsdp', axis=1, tiled=True)]
    reduce_sum x14 -> x0, other arithmetic: 31.7 us -> none  [the longest x1 14.5 us: local(): centred = conv_out - jnp.mean(conv_out, axis=3, keepdims=True)]
  transfers between devices with their start and end apart: 6 -> 0, of which waited for: 5 -> 0; matrix products, arithmetic and copies ran while one was open for 2% -> 0% of each run, Pallas kernels for 0% -> 0%
where the time goes in v2:
time: 166 us; the launch traced here: 164 us
  Pallas kernels  156 us (94%)
  local copies, waits for them, and re-layouts  6.4 us (4%)
  between operations  2.5 us (2%)
    pallas_call x5, Pallas kernels, call(): pl.pallas_call(kernel, out_shape=[jax.ShapeDtypeStruct(s, d) for s, d in...  156 us
    unnamed x19, local copies, waits for them, and re-layouts  5.31 us

profile of v2, /device:TPU:6, one launch (start us, length us, event | category | flops | bytes accessed | tf_op | source)
XLA Modules:
  0.0 164.5 jit_solution(16273966401233813503)
XLA Ops:
  0.6 0.0 copy-start.2
  0.6 0.0 copy-start.3
  0.7 0.8 copy-done.3
  1.5 0.0 copy-start.5
  1.5 0.7 copy-done.5
  2.2 0.0 copy-start.6
  2.2 0.7 copy-done.6
  2.9 0.0 copy-start.4
  2.9 0.0 copy-start.7
  2.9 17.9 %shard_map.134.full = f32[56,3072]{1,0:T(8,128)S(1)} custom-call(f32[49,192]{1,0:T(8,128)S(1)} %copy-done.3, f32[1,192]{1,0:T(1,128)S(1)} %bitcast.9, f32[1,192]{1,0:T(1,128)S(1)} %bitcast.10), custom_call_target="tpu_custom_call" | custom-call | tf_op jit(solution)/shard_map/pallas_call | solution.py:563
  20.8 0.0 copy-start
  20.8 1.1 copy-done
  22.0 0.0 copy-start.1
  22.0 7.0 %shard_map.135 = (f32[2,8,8,3072]{3,2,1,0:T(8,128)S(1)}, f32[2,8,8,128]{3,2,1,0:T(8,128)S(1)}, f32[2,3072]{1,0:T(2,128)S(1)}, f32[2,3072]{1,0:T(2,128)S(1)}, f32[2,128]{1,0:T(2,128)S(1)}) custom-call(bf16[2,8,8,3072]{3,2,1,0:T(8,128)(2,1)S(1)} %copy-done, f32[56,3072]{1,0:T(8,128)S(1)} %shard_map.134.full), custom_call_target="tpu_custom_call" | custom-call | tf_op jit(solution)/shard_map/pallas_call | solution.py:563
  29.0 0.0 copy-done.2
  29.0 0.0 copy-done.4
  29.0 0.0 copy-done.7
  29.0 56.9 %shard_map.136 = (f32[2,3072]{1,0:T(2,128)S(1)}, f32[192,512]{1,0:T(8,128)S(1)}, f32[1,192]{1,0:T(1,128)S(1)}, f32[1,128]{1,0:T(1,128)S(1)}, f32[2,512]{1,0:T(2,128)S(1)}) custom-call(f32[2,3072]{1,0:T(2,128)S(1)} %get-tuple-element.25.normed_ref, f32[1,192]{1,0:T(1,128)S(1)} %bitcast.11, bf16[192,512]{1,0:T(8,128)(2,1)S(1)} %copy-done.2, ...), custom_call_target="tpu_custom_call" | custom-call | tf_op jit(solution)/shard_map/pallas_call | solution.py:563
  85.8 0.0 copy-done.1
  85.9 12.0 %shard_map.137 = (bf16[2,8,8,3072]{3,2,1,0:T(8,128)(2,1)}, f32[16,56,192]{2,1,0:T(8,128)S(1)}) custom-call(bf16[2,8,8,3072]{3,2,1,0:T(8,128)(2,1)S(1)} %copy-done.1, f32[2,8,8,3072]{3,2,1,0:T(8,128)S(1)} %get-tuple-element.22.z_ref, f32[2,8,8,128]{3,2,1,0:T(8,128)S(1)} %get-tuple-element.23.inv_ref, f32[56,3072]{1,0:T(8,128)S(1)} %shard_map.134.full, ...), custom_call_target="tpu_custom_call" | custom-call | tf_op jit(solution)/shard_map/pallas_call | solution.py:563
  97.8 61.8 %shard_map.138 = (f32[56,192]{1,0:T(8,128)S(1)}, f32[192,512]{1,0:T(8,128)S(1)}) custom-call(f32[16,56,192]{2,1,0:T(8,128)S(1)} %get-tuple-element.29.blocks_ref, f32[1,192]{1,0:T(1,128)S(1)} %get-tuple-element.30.headgrad_ref, f32[192,512]{1,0:T(8,128)S(1)} %get-tuple-element.31.projgrad_ref), custom_call_target="tpu_custom_call" | custom-call | tf_op jit(solution)/shard_map/pallas_call | solution.py:563
  159.6 0.5 slice.15
  160.8 0.6 fusion
  161.4 0.6 copy.18
  162.0 0.7 copy.19
  162.7 0.6 copy.20
Async XLA Ops:
  0.6 28.3 %copy-start.2 = (bf16[192,512]{1,0:T(8,128)(2,1)S(1)}, bf16[192,512]{1,0:T(8,128)(2,1)}, u32[]{:S(2)}) copy-start(bf16[192,512]{1,0:T(8,128)(2,1)} %proj_ref.1) | copy-start | bytes 589828
  0.6 0.9 copy-start.3
  1.5 0.7 copy-start.5
  2.2 0.7 copy-start.6
  2.9 26.1 %copy-start.4 = (bf16[2,512]{1,0:T(2,128)(2,1)S(1)}, bf16[2,512]{1,0:T(2,128)(2,1)}, u32[]{:S(2)}) copy-start(bf16[2,512]{1,0:T(2,128)(2,1)} %text_ref.1) | copy-start | bytes 6148
  2.9 26.1 %copy-start.7 = (f32[192]{0:T(256)S(1)}, f32[192]{0:T(256)}, u32[]{:S(2)}) copy-start(f32[192]{0:T(256)} %param.11) | copy-start | bytes 2308
  20.8 1.1 copy-start
  22.0 63.9 %copy-start.1 = (bf16[2,8,8,3072]{3,2,1,0:T(8,128)(2,1)S(1)}, bf16[2,8,8,3072]{3,2,1,0:T(8,128)(2,1)}, u32[]{:S(2)}) copy-start(bf16[2,8,8,3072]{3,2,1,0:T(8,128)(2,1)} %images.3) | copy-start | bytes 2359300

commit v3 on v2

v3 whole, which is shorter than its diff:
```python
import jax
import jax.numpy as jnp
from jax import lax
from jax.experimental import pallas as pl
from jax.experimental.pallas import tpu as pltpu
from jax.sharding import PartitionSpec as P

KERNEL = 7
MAP_SIDE = 8
LOGIT_SCALE = 14.0
EPSILON = 1e-06
MESH = pl.DeviceIdType.MESH
F32 = jnp.float32
BF16 = jnp.bfloat16
N_DP = 32
N_FSDP = 16
IMGS = 2
CHANNELS = 3072
SHARD = 192
EMBED = 512
ROWS = 56
BIAS_ROW, BLOCK_ROW, HEAD_ROW, LOSS_ROW = 49, 50, 51, 52
BLOCKS = CHANNELS // 128
VMEM_SPEC = pl.BlockSpec(memory_space=pltpu.VMEM)


def contract(left, right, left_dim, right_dim):
    return lax.dot_general(
        left, right, (((left_dim,), (right_dim,)), ((), ())), preferred_element_type=F32
    )


def copy_to(axis, peer, src, dst, send_sem, recv_sem):
    return pltpu.make_async_remote_copy(
        src_ref=src,
        dst_ref=dst,
        send_sem=send_sem,
        recv_sem=recv_sem,
        device_id={axis: peer},
        device_id_type=MESH,
    )


def loop(low, high, body):
    def step(t, carry):
        body(t)
        return carry

    lax.fori_loop(low, high, step, 0)


def greet(me_f, me_d):
    barrier = pltpu.get_barrier_semaphore()

    def signal(axis, me, count):
        def body(t):
            peer = lax.rem(me + t, count)
            pl.semaphore_signal(barrier, inc=1, device_id={axis: peer}, device_id_type=MESH)

        loop(1, count, body)

    signal("dp", me_d, N_DP)
    signal("fsdp", me_f, N_FSDP)


def greeted():
    pl.semaphore_wait(pltpu.get_barrier_semaphore(), N_FSDP + N_DP - 2)


class Exchange:
    def __init__(self, axis, count, me, source, dst, send_sem, recv_sem):
        self.axis, self.count, self.me = axis, count, me
        self.source, self.dst, self.send_sem, self.recv_sem = source, dst, send_sem, recv_sem

    def _each(self, act):
        def body(t):
            act(t, lax.rem(self.me + t, self.count))

        loop(1, self.count, body)

    def start(self):
        def act(t, peer):
            copy_to(
                self.axis, peer, self.source(peer), self.dst.at[self.me],
                self.send_sem.at[t], self.recv_sem.at[self.me],
            ).start()

        self._each(act)

    def wait_recv(self):
        def act(t, peer):
            copy_to(
                self.axis, peer, self.source(peer), self.dst.at[peer],
                self.send_sem.at[t], self.recv_sem.at[peer],
            ).wait_recv()

        self._each(act)

    def wait_recv_from(self, sender):
        copy_to(
            self.axis, sender, self.source(sender), self.dst.at[sender],
            self.send_sem.at[0], self.recv_sem.at[sender],
        ).wait_recv()

    def wait_send(self):
        def act(t, peer):
            copy_to(
                self.axis, peer, self.source(peer), self.dst.at[self.me],
                self.send_sem.at[t], self.recv_sem.at[self.me],
            ).wait_send()

        self._each(act)


def join_pairs(read, write):
    for p in range(N_FSDP // 2):
        write(p, jnp.concatenate([read(2 * p), read(2 * p + 1)], axis=1))


def shifted(value, amount):
    if amount == 0:
        return value
    place = lax.broadcasted_iota(jnp.int32, value.shape, 0)
    rolled = pltpu.roll(value, amount % MAP_SIDE, 0)
    inside = place >= amount if amount > 0 else place < MAP_SIDE + amount
    return jnp.where(inside, rolled, 0.0)


def lanes_of(block):
    return pl.ds(pl.multiple_of(block * 128, 128), 128)


PAIRS = N_FSDP // 2
PROJ_OWNERS = SHARD // 8
SMALL_OWNERS = ROWS // 8


def pair_lanes(p):
    return pl.ds(pl.multiple_of(p * (2 * SHARD), 128), 2 * SHARD)


def stack(ref, count):
    return jnp.concatenate([ref[k] for k in range(count)], axis=0)


def total(ref, count):
    out = ref[0]
    for k in range(1, count):
        out = out + ref[k]
    return out


def spread(ref, value):
    for k in range(ref.shape[0]):
        ref[k] = value[IMGS * k : IMGS * (k + 1)]


def forward_block(block, images, full, z, sums, isum):
    margin = KERNEL // 2
    lanes = lanes_of(block)
    for b in range(IMGS):
        rows = [images[b, i, :, lanes].astype(F32) for i in range(MAP_SIDE)]
        pixels = rows[0]
        for i in range(1, MAP_SIDE):
            pixels = pixels + rows[i]
        isum[b, :, lanes] = pixels
        bias = jnp.broadcast_to(full[pl.ds(BIAS_ROW, 1), lanes], (MAP_SIDE, 128))
        acc = [bias] * MAP_SIDE
        for s in range(KERNEL):
            cols = [shifted(row, margin - s) for row in rows]
            for r in range(KERNEL):
                tap = jnp.broadcast_to(full[pl.ds(r * KERNEL + s, 1), lanes], (MAP_SIDE, 128))
                for i in range(MAP_SIDE):
                    if 0 <= i + r - margin < MAP_SIDE:
                        acc[i] = acc[i] + cols[i + r - margin] * tap
        for i in range(MAP_SIDE):
            z[b, i, :, lanes] = acc[i]
            sums[b, i] += acc[i]


def forward_norm(full, z, inv, zsum, sums, isum, pooled):
    mean = jnp.sum(sums[...], axis=3, keepdims=True) * (1.0 / CHANNELS)
    inv[...] = jnp.broadcast_to(mean, sums.shape)
    sums[...] = jnp.zeros_like(sums)

    def centre(block):
        lanes = lanes_of(block)
        value = z[:, :, :, lanes] - inv[...]
        z[:, :, :, lanes] = value
        sums[...] += value * value

    loop(0, BLOCKS, centre)
    var = jnp.sum(sums[...], axis=3, keepdims=True) * (1.0 / CHANNELS)
    inv[...] = jnp.broadcast_to(lax.rsqrt(var + EPSILON), sums.shape)

    def norm(block):
        lanes = lanes_of(block)
        value = z[:, :, :, lanes] * inv[...]
        z[:, :, :, lanes] = value
        zs = jnp.sum(jnp.sum(value, axis=1), axis=1)
        zsum[:, lanes] = zs
        gain = full[pl.ds(BLOCK_ROW, 1), lanes]
        img = jnp.sum(isum[:, :, lanes], axis=1)
        pooled[:, lanes] = (img + zs * gain) * (1.0 / (MAP_SIDE * MAP_SIDE))

    loop(0, BLOCKS, norm)
    value = pooled[...]
    centred = value - jnp.mean(value, axis=1, keepdims=True)
    inverse = lax.rsqrt(jnp.mean(centred * centred, axis=1, keepdims=True) + EPSILON)
    return centred * inverse, inverse


def backward_block(block, images, z, inv, full, dh, dn, sums, mean1, grads, gimg):
    margin = KERNEL // 2
    lanes = lanes_of(block)
    maps, pixels, acc = [], [], []
    bias = None
    for b in range(IMGS):
        row = jnp.broadcast_to(dn[pl.ds(b, 1), lanes], (MAP_SIDE, 128)) - jnp.broadcast_to(
            mean1[pl.ds(b, 1), :], (MAP_SIDE, 128)
        )
        hidden = jnp.broadcast_to(dh[pl.ds(b, 1), lanes], (MAP_SIDE, 128))
        for i in range(MAP_SIDE):
            value = inv[b, i] * (row - z[b, i, :, lanes] * sums[b, i])
            maps.append(value)
            bias = value if bias is None else bias + value
            pixels.append(images[b, i, :, lanes].astype(F32))
            acc.append(hidden)
    grads[pl.ds(BIAS_ROW, 1), lanes] = jnp.sum(bias, axis=0, keepdims=True)
    for s in range(KERNEL):
        cols = [shifted(value, s - margin) for value in maps]
        for r in range(KERNEL):
            tap = jnp.broadcast_to(full[pl.ds(r * KERNEL + s, 1), lanes], (MAP_SIDE, 128))
            grad = None
            for b in range(IMGS):
                for i in range(MAP_SIDE):
                    if 0 <= i - r + margin < MAP_SIDE:
                        col = cols[b * MAP_SIDE + i - r + margin]
                        k = b * MAP_SIDE + i
                        acc[k] = acc[k] + col * tap
                        term = col * pixels[k]
                        grad = term if grad is None else grad + term
            grads[pl.ds(r * KERNEL + s, 1), lanes] = jnp.sum(grad, axis=0, keepdims=True)
    for b in range(IMGS):
        for i in range(MAP_SIDE):
            gimg[b, i, :, lanes] = acc[b * MAP_SIDE + i].astype(BF16)


def step_kernel(
    images_hbm, w_hbm, bias_hbm, gain_hbm, head_hbm, proj_hbm, text_hbm,
    gimg_hbm, small_out, proj_out, gtext_out,
    images, w_in, bias_in, gain_in, head_in, proj_in, text_in,
    pack, held, full, z, inv, zsum, sums, isum, pooled,
    normed_s, normed_r, part_s, part_r, img_s, img_r, row_s, row_r, dimg_s, dimg_r,
    demb_s, demb_r, dn_s, dn_r, text_s, text_r, col_s, col_r, dcap_s, dcap_r,
    dnormed, projgrad, grads, dh, dn, mean1, gimg, blocks_s, blocks_r,
    small, proj_r, small_r, proj_mine, small_mine, proj_all, small_all,
    load_sem, fs, fr, ds, dr, ps, pr, ss, sr, gs, gr,
):
    me_f, me_d = lax.axis_index("fsdp"), lax.axis_index("dp")
    my_pair = lax.div(me_f, 2)
    greet(me_f, me_d)
    loads = [
        pltpu.make_async_copy(src, dst, load_sem.at[n])
        for n, (src, dst) in enumerate(
            (
                (w_hbm, w_in), (bias_hbm, bias_in), (gain_hbm, gain_in), (text_hbm, text_in),
                (images_hbm, images), (head_hbm, head_in), (proj_hbm, proj_in),
            )
        )
    ]
    for load in loads:
        load.start()

    def fex(n, source, dst):
        return Exchange("fsdp", N_FSDP, me_f, source, dst, fs.at[n], fr.at[n])

    def dex(n, source, dst):
        return Exchange("dp", N_DP, me_d, source, dst, ds.at[n], dr.at[n])

    sums[...] = jnp.zeros_like(sums)
    for load in loads[:4]:
        load.wait()
    rows = jnp.concatenate(
        [w_in[...], bias_in[...], gain_in[...], jnp.zeros((ROWS - 51, SHARD), F32)], axis=0
    )
    pack[...] = rows
    held[me_f] = rows
    text = text_in[...].astype(F32)
    text_scale = lax.rsqrt(jnp.sum(text * text, axis=1, keepdims=True) + EPSILON)
    text_f = text * text_scale
    text_unit = text_f.astype(BF16)
    text_s[...] = text_unit
    text_r[me_d] = text_unit
    greeted()
    x_pack = fex(7, lambda peer: pack, held)
    x_pack.start()
    x_text = dex(0, lambda peer: text_s, text_r)
    x_text.start()
    for load in loads[4:]:
        load.wait()

    def forward_pair(t):
        p = lax.rem(my_pair - t + PAIRS, PAIRS)
        for c in range(2):

            @pl.when(2 * p + c != me_f)
            def _():
                x_pack.wait_recv_from(2 * p + c)

        full[:, pair_lanes(p)] = jnp.concatenate([held[2 * p], held[2 * p + 1]], axis=1)
        loop(0, 3, lambda k: forward_block(3 * p + k, images, full, z, sums, isum))

    loop(0, PAIRS, forward_pair)
    pool_normed, pool_inverse = forward_norm(full, z, inv, zsum, sums, isum, pooled)

    for p in range(PAIRS):
        value = pool_normed[:, 384 * p : 384 * (p + 1)]
        normed_s[2 * p] = value[:, :SHARD]
        normed_s[2 * p + 1] = value[:, SHARD:]
    pooled[...] = pool_normed
    normed_r[me_f] = normed_s[me_f]
    x_norm = fex(0, lambda peer: normed_s.at[peer], normed_r)
    x_norm.start()
    x_text.wait_recv()
    text_cols = stack(text_r, N_DP)
    x_norm.wait_recv()
    normed = stack(normed_r, N_FSDP)
    head = head_in[...]
    query = (normed * head).astype(BF16)
    part = jnp.dot(query, proj_in[...], preferred_element_type=F32)
    spread(part_s, part)
    part_r[me_f] = part_s[me_f]
    x_part = fex(1, lambda peer: part_s.at[peer], part_r)
    x_part.start()
    x_part.wait_recv()
    embedding = total(part_r, N_FSDP)
    image_scale = lax.rsqrt(jnp.sum(embedding * embedding, axis=1, keepdims=True) + EPSILON)
    image_f = embedding * image_scale
    image_unit = image_f.astype(BF16)
    img_s[...] = image_unit
    img_r[me_f] = image_unit
    x_img = fex(2, lambda peer: img_s, img_r)
    x_img.start()
    diagonal = LOGIT_SCALE * jnp.sum(image_unit.astype(F32) * text_unit.astype(F32))

    n_row, n_col = N_FSDP * IMGS, N_DP * IMGS
    eye = (
        lax.broadcasted_iota(jnp.int32, (n_row, 128), 0)
        == lax.broadcasted_iota(jnp.int32, (n_row, 128), 1)
    )
    x_img.wait_recv()
    image_rows = stack(img_r, N_FSDP)
    logits = LOGIT_SCALE * contract(image_rows, text_cols, 1, 1)
    exps = jnp.exp(logits)
    col_part = jnp.sum(exps, axis=0, keepdims=True)
    col_flat = jnp.concatenate([col_part, jnp.zeros((1, 128 - n_col), F32)], axis=1)
    col_s[...] = col_flat
    col_r[me_d] = col_flat
    x_col = dex(1, lambda peer: col_s, col_r)
    x_col.start()
    row_part = jnp.sum(exps, axis=1, keepdims=True)
    row_flat = jnp.sum(jnp.where(eye, row_part, 0.0), axis=0, keepdims=True)
    row_s[...] = row_flat
    row_r[me_f] = row_flat
    x_row = fex(3, lambda peer: row_s, row_r)
    x_row.start()
    x_row.wait_recv()
    row_sum = total(row_r, N_FSDP)
    row_lse = jnp.log(jnp.sum(jnp.where(eye, row_sum, 0.0), axis=1, keepdims=True))
    row_term = jnp.exp(logits - row_lse)
    at_row = lax.broadcasted_iota(jnp.int32, (n_row, n_col), 0)
    at_col = lax.broadcasted_iota(jnp.int32, (n_row, n_col), 1)
    pair = jnp.where(
        (at_row - IMGS * me_f == at_col - IMGS * me_d)
        & (at_row >= IMGS * me_f)
        & (at_row < IMGS * me_f + IMGS),
        2.0,
        0.0,
    )
    x_col.wait_recv()
    col_lse = jnp.log(total(col_r, N_DP)[:, :n_col])
    weights = (row_term + jnp.exp(logits - col_lse) - pair).astype(BF16)
    dimg = jnp.dot(weights, text_cols, preferred_element_type=F32)
    spread(dimg_s, dimg)
    dimg_r[me_f] = dimg_s[me_f]
    x_dimg = fex(4, lambda peer: dimg_s.at[peer], dimg_r)
    x_dimg.start()
    dcap = contract(weights, image_rows, 0, 0)
    spread(dcap_s, dcap)
    dcap_r[me_d] = dcap_s[me_d]
    x_dcap = dex(2, lambda peer: dcap_s.at[peer], dcap_r)
    x_dcap.start()
    loss_part = (
        jnp.sum(row_lse) * (1.0 / N_FSDP) + jnp.sum(col_lse) * (1.0 / N_DP) - 2.0 * diagonal
    )
    x_dimg.wait_recv()
    d_image = 7.0 * total(dimg_r, N_FSDP)
    d_embedding = (
        image_scale * (d_image - image_f * jnp.sum(image_f * d_image, axis=1, keepdims=True))
    ).astype(BF16)
    demb_s[...] = d_embedding
    demb_r[me_f] = d_embedding
    x_demb = fex(5, lambda peer: demb_s, demb_r)
    x_demb.start()
    x_demb.wait_recv()
    demb = stack(demb_r, N_FSDP)
    d_query = contract(demb, proj_in[...], 1, 1)
    spread(dn_s, d_query * head)
    dn_r[me_f] = dn_s[me_f]
    x_dn = fex(6, lambda peer: dn_s.at[peer], dn_r)
    x_dn.start()
    head_grad = jnp.sum(d_query * normed, axis=0, keepdims=True)
    projgrad[...] = contract(query, demb, 0, 0)

    first = PROJ_OWNERS
    last = PROJ_OWNERS + SMALL_OWNERS

    def proj_rows(k):
        return pl.ds(pl.multiple_of(k * 8, 8), 8)

    def small_rows(k):
        return pl.ds(pl.multiple_of((k - first) * 8, 8), 8)

    def peers(act):
        def body(t):
            act(t, lax.rem(me_d + t, N_DP))

        loop(1, N_DP, body)

    def proj_copy(t, peer, to):
        return copy_to("dp", peer, projgrad.at[proj_rows(to)], proj_r.at[me_d], ps.at[t], pr.at[me_d])

    def small_copy(t, peer, to):
        return copy_to("dp", peer, small.at[small_rows(to)], small_r.at[me_d], ss.at[t], sr.at[me_d])

    def start_proj(t, peer):
        @pl.when(peer < first)
        def _():
            proj_copy(t, peer, peer).start()

    peers(start_proj)

    x_dn.wait_recv()

    def write(p, value):
        dnormed[:, 384 * p : 384 * (p + 1)] = value

    join_pairs(lambda k: dn_r[k], write)

    normed = pooled[...]
    d_normed = dnormed[...]
    d_pooled = pool_inverse * (
        d_normed
        - jnp.mean(d_normed, axis=1, keepdims=True)
        - normed * jnp.mean(d_normed * normed, axis=1, keepdims=True)
    )
    d_hidden = d_pooled * (1.0 / (MAP_SIDE * MAP_SIDE))
    dh[...] = d_hidden
    d_norm = d_hidden * full[BLOCK_ROW : BLOCK_ROW + 1, :]
    dn[...] = d_norm
    grads[ROWS - 8 :, :] = jnp.zeros((8, CHANNELS), F32)
    grads[BLOCK_ROW : BLOCK_ROW + 1, :] = jnp.sum(d_hidden * zsum[...], axis=0, keepdims=True)
    grads[LOSS_ROW : LOSS_ROW + 1, :] = jnp.full((1, CHANNELS), loss_part, F32)
    mean1[...] = jnp.broadcast_to(jnp.mean(d_norm, axis=1, keepdims=True), mean1.shape)
    sums[...] = jnp.zeros_like(sums)

    def project(block):
        lanes = lanes_of(block)
        for b in range(IMGS):
            row = jnp.broadcast_to(dn[pl.ds(b, 1), lanes], (MAP_SIDE, 128))
            for i in range(MAP_SIDE):
                sums[b, i] += row * z[b, i, :, lanes]

    loop(0, BLOCKS, project)
    mean2 = jnp.sum(sums[...], axis=3, keepdims=True) * (1.0 / CHANNELS)
    sums[...] = jnp.broadcast_to(mean2, sums.shape)

    def block_copy(owner):
        return copy_to(
            "fsdp", owner, blocks_s.at[owner], blocks_r.at[me_f], fs.at[8, owner], fr.at[8, me_f]
        )

    def backward_pair(t):
        p = lax.rem(my_pair + t, PAIRS)
        loop(
            0, 3,
            lambda k: backward_block(
                3 * p + k, images, z, inv, full, dh, dn, sums, mean1, grads, gimg
            ),
        )
        value = grads[:, pair_lanes(p)]
        for c in range(2):
            owner = 2 * p + c
            blocks_s[owner] = value[:, SHARD * c : SHARD * (c + 1)]

            @pl.when(owner != me_f)
            def _():
                block_copy(owner).start()

    loop(1, PAIRS + 1, backward_pair)
    store = pltpu.make_async_copy(gimg, gimg_hbm, load_sem.at[7])
    store.start()
    blocks_r[me_f] = blocks_s[me_f]

    def senders(act):
        loop(1, N_FSDP, lambda t: act(lax.rem(me_f - t + N_FSDP, N_FSDP)))

    senders(
        lambda s: copy_to(
            "fsdp", s, blocks_s.at[s], blocks_r.at[s], fs.at[8, s], fr.at[8, s]
        ).wait_recv()
    )
    small[...] = total(blocks_r, N_FSDP)
    small[HEAD_ROW : HEAD_ROW + 1, :] = head_grad

    def start_small(t, peer):
        @pl.when((peer >= first) & (peer < last))
        def _():
            small_copy(t, peer, peer).start()

    peers(start_small)

    def all_copy(t, peer, sender, mine, everyone, slot):
        return copy_to("dp", peer, mine, everyone.at[slot], gs.at[t], gr.at[sender])

    @pl.when(me_d < first)
    def _():
        proj_r[me_d] = projgrad[proj_rows(me_d), :]

        def wait(t, peer):
            copy_to(
                "dp", peer, projgrad.at[proj_rows(0)], proj_r.at[peer], ps.at[t], pr.at[peer]
            ).wait_recv()

        peers(wait)
        out = total(proj_r, N_DP).astype(BF16)
        proj_mine[...] = out
        proj_all[me_d] = out
        peers(lambda t, peer: all_copy(t, peer, me_d, proj_mine, proj_all, me_d).start())

    @pl.when((me_d >= first) & (me_d < last))
    def _():
        small_r[me_d] = small[small_rows(me_d), :]

        def wait(t, peer):
            copy_to(
                "dp", peer, small.at[small_rows(first)], small_r.at[peer], ss.at[t], sr.at[peer]
            ).wait_recv()

        peers(wait)
        out = total(small_r, N_DP)
        small_mine[...] = out
        small_all[me_d - first] = out
        peers(lambda t, peer: all_copy(t, peer, me_d, small_mine, small_all, me_d - first).start())

    x_dcap.wait_recv()
    d_caption = 7.0 * total(dcap_r, N_DP)
    gtext_out[...] = text_scale * (
        d_caption - text_f * jnp.sum(text_f * d_caption, axis=1, keepdims=True)
    )

    def wait_all(t, peer):
        @pl.when(peer < first)
        def _():
            all_copy(t, peer, peer, proj_mine, proj_all, peer).wait_recv()

        @pl.when((peer >= first) & (peer < last))
        def _():
            all_copy(t, peer, peer, small_mine, small_all, peer - first).wait_recv()

    peers(wait_all)
    for k in range(PROJ_OWNERS):
        proj_out[8 * k : 8 * (k + 1), :] = proj_all[k].astype(F32)
    for k in range(SMALL_OWNERS):
        small_out[8 * k : 8 * (k + 1), :] = small_all[k]

    store.wait()
    for ex in (x_pack, x_text, x_norm, x_part, x_img, x_col, x_row, x_dimg, x_dcap, x_demb, x_dn):
        ex.wait_send()

    def drain_block(owner):
        block_copy(owner).wait_send()

    senders(drain_block)

    def drain(t, peer):
        @pl.when(peer < first)
        def _():
            proj_copy(t, peer, peer).wait_send()

        @pl.when((peer >= first) & (peer < last))
        def _():
            small_copy(t, peer, peer).wait_send()

        @pl.when(me_d < first)
        def _():
            all_copy(t, peer, me_d, proj_mine, proj_all, me_d).wait_send()

        @pl.when((me_d >= first) & (me_d < last))
        def _():
            all_copy(t, peer, me_d, small_mine, small_all, me_d - first).wait_send()

    peers(drain)


def dma(*shape):
    return pltpu.SemaphoreType.DMA(shape)


def local(images, dw_weight, dw_bias, block_gain, head_gain, projection, text):
    V = pltpu.VMEM
    maps = (IMGS, MAP_SIDE, MAP_SIDE, CHANNELS)
    lanes = (IMGS, MAP_SIDE, MAP_SIDE, 128)
    wide = (IMGS, CHANNELS)
    two = (IMGS, EMBED)

    def f_blocks(shape, kind):
        return V((N_FSDP,) + shape, kind)

    def d_blocks(shape, kind):
        return V((N_DP,) + shape, kind)

    inputs = (images, dw_weight, dw_bias[None], block_gain[None], head_gain[None], projection, text)
    grad_images, sums, sum_proj, grad_text = pl.pallas_call(
        step_kernel,
        out_shape=[
            jax.ShapeDtypeStruct(shape, kind)
            for shape, kind in ((maps, BF16), ((ROWS, SHARD), F32), ((SHARD, EMBED), F32), (two, F32))
        ],
        in_specs=[pl.BlockSpec(memory_space=pl.ANY)] * len(inputs),
        out_specs=[pl.BlockSpec(memory_space=pl.ANY)] + [VMEM_SPEC] * 3,
        scratch_shapes=[
            V(maps, BF16), V((KERNEL * KERNEL, SHARD), F32), V((1, SHARD), F32), V((1, SHARD), F32),
            V((1, SHARD), F32), V((SHARD, EMBED), BF16), V(two, BF16),
            V((ROWS, SHARD), F32), f_blocks((ROWS, SHARD), F32), V((ROWS, CHANNELS), F32),
            V(maps, F32), V(lanes, F32), V(wide, F32), V(lanes, F32),
            V((IMGS, MAP_SIDE, CHANNELS), F32), V(wide, F32),
            f_blocks((IMGS, SHARD), F32), f_blocks((IMGS, SHARD), F32),
            f_blocks(two, F32), f_blocks(two, F32),
            V(two, BF16), f_blocks(two, BF16),
            V((1, 128), F32), f_blocks((1, 128), F32),
            f_blocks(two, F32), f_blocks(two, F32),
            V(two, BF16), f_blocks(two, BF16),
            f_blocks((IMGS, SHARD), F32), f_blocks((IMGS, SHARD), F32),
            V(two, BF16), d_blocks(two, BF16),
            V((1, 128), F32), d_blocks((1, 128), F32),
            d_blocks(two, F32), d_blocks(two, F32),
            V(wide, F32), V((SHARD, EMBED), F32), V((ROWS, CHANNELS), F32), V(wide, F32),
            V(wide, F32), V((IMGS, 128), F32), V(maps, BF16),
            f_blocks((ROWS, SHARD), F32), f_blocks((ROWS, SHARD), F32),
            V((ROWS, SHARD), F32), d_blocks((8, EMBED), F32), d_blocks((8, SHARD), F32),
            V((8, EMBED), BF16), V((8, SHARD), F32),
            V((PROJ_OWNERS, 8, EMBED), BF16), V((SMALL_OWNERS, 8, SHARD), F32),
            dma(8), dma(9, N_FSDP), dma(9, N_FSDP), dma(3, N_DP), dma(3, N_DP),
            dma(N_DP), dma(N_DP), dma(N_DP), dma(N_DP), dma(N_DP), dma(N_DP),
        ],
        compiler_params=pltpu.CompilerParams(
            vmem_limit_bytes=48 * 1024 * 1024, collective_id=0, has_side_effects=True
        ),
    )(*inputs)
    return (
        sums[LOSS_ROW, 0] / (2.0 * N_DP * N_FSDP * IMGS),
        grad_images,
        sums[: KERNEL * KERNEL],
        sums[BIAS_ROW],
        sums[BLOCK_ROW],
        sums[HEAD_ROW],
        sum_proj,
        grad_text,
    )


def solution(mesh):
    return jax.shard_map(
        local,
        mesh=mesh,
        in_specs=(
            P(("dp", "fsdp"), None, None, None),
            P(None, "fsdp"),
            P("fsdp"),
            P("fsdp"),
            P("fsdp"),
            P("fsdp", None),
            P(("dp", "fsdp"), None),
        ),
        out_specs=(
            P(),
            P(("dp", "fsdp"), None, None, None),
            P(None, "fsdp"),
            P("fsdp"),
            P("fsdp"),
            P("fsdp"),
            P("fsdp", None),
            P(("dp", "fsdp"), None),
        ),
        check_vma=False,
    )
```

time: 166 us -> 132 us (0.80)
  the two profiles are of different devices: /device:TPU:6 before, /device:TPU:33 now
where the time goes in v3:
time: 132 us
  Pallas kernels  122 us (92%)
  local copies, waits for them, and re-layouts  7.5 us (6%)
  between operations  2.47 us (2%)
    pallas_call x1, Pallas kernels, local(): pl.pallas_call(step_kernel, out_shape=[jax.ShapeDtypeStruct(shape, kind)...  122 us
    unnamed x18, local copies, waits for them, and re-layouts  6.41 us

profile of v3, /device:TPU:33, one launch (start us, length us, event | category | flops | bytes accessed | tf_op | source)
XLA Modules:
  0.0 132.0 jit_solution(531097638973018035)
XLA Ops:
  0.6 0.0 copy-start.5
  0.6 0.0 copy-start.6
  0.7 0.0 copy-start.3
  0.7 0.0 copy-start.4
  0.7 0.6 copy-done.5
  1.3 0.0 copy-done.6
  1.3 0.0 copy-done.3
  1.3 0.0 copy-done.4
  1.4 0.0 copy-start
  1.4 1.1 copy-done
  2.5 0.0 copy-start.1
  2.5 0.9 copy-done.1
  3.4 0.0 copy-start.2
  3.4 0.8 copy-done.2
  4.2 122.0 %shard_map.134 = (bf16[2,8,8,3072]{3,2,1,0:T(8,128)(2,1)S(1)}, f32[56,192]{1,0:T(8,128)S(1)}, f32[192,512]{1,0:T(8,128)S(1)}, f32[2,512]{1,0:T(2,128)S(1)}) custom-call(bf16[2,8,8,3072]{3,2,1,0:T(8,128)(2,1)S(1)} %copy-done, f32[49,192]{1,0:T(8,128)S(1)} %copy-done.2, f32[1,192]{1,0:T(1,128)S(1)} %bitcast.9, f32[1,192]{1,0:T(1,128)S(1)} %bitcast.10, ...), custom_call_target="tpu_custom_call" | custom-call | tf_op jit(solution)/shard_map/pallas_call | solution.py:625
  126.3 0.5 slice.15
  127.5 0.6 fusion
  128.0 0.9 copy.19
  128.9 0.6 copy.20
  129.5 0.7 copy.21
  130.3 0.6 copy.22
Async XLA Ops:
  0.6 0.7 copy-start.5
  0.6 0.7 copy-start.6
  0.7 0.7 copy-start.3
  0.7 0.7 copy-start.4
  1.4 1.1 copy-start
  2.5 0.9 copy-start.1
  3.4 0.8 copy-start.2

commit v4 on v3

--- a/solution.py
+++ b/solution.py
@@ -72,44 +72,31 @@
         self.axis, self.count, self.me = axis, count, me
         self.source, self.dst, self.send_sem, self.recv_sem = source, dst, send_sem, recv_sem
 
-    def _each(self, act):
+    def start(self):
         def body(t):
-            act(t, lax.rem(self.me + t, self.count))
-
-        loop(1, self.count, body)
-
-    def start(self):
-        def act(t, peer):
+            offset = 1 + lax.rem(t + self.count // 2 - 2, self.count - 1)
+            peer = lax.rem(self.me + offset, self.count)
             copy_to(
-                self.axis, peer, self.source(peer), self.dst.at[self.me],
-                self.send_sem.at[t], self.recv_sem.at[self.me],
+                self.axis, peer, self.source(peer), self.dst.at[self.me], self.send_sem, self.recv_sem
             ).start()
 
-        self._each(act)
+        loop(0, self.count - 1, body)
 
     def wait_recv(self):
-        def act(t, peer):
-            copy_to(
-                self.axis, peer, self.source(peer), self.dst.at[peer],
-                self.send_sem.at[t], self.recv_sem.at[peer],
-            ).wait_recv()
-
-        self._each(act)
-
-    def wait_recv_from(self, sender):
-        copy_to(
-            self.axis, sender, self.source(sender), self.dst.at[sender],
-            self.send_sem.at[0], self.recv_sem.at[sender],
-        ).wait_recv()
+        wait_blocks(self.axis, self.count, self.me, self.dst, self.count - 1, None, self.recv_sem)
 
     def wait_send(self):
-        def act(t, peer):
-            copy_to(
-                self.axis, peer, self.source(peer), self.dst.at[self.me],
-                self.send_sem.at[t], self.recv_sem.at[self.me],
-            ).wait_send()
-
-        self._each(act)
+        wait_blocks(self.axis, self.count, self.me, self.dst, self.count - 1, self.send_sem, None)
+
+
+def wait_blocks(axis, count, me, like, blocks, send_sem, recv_sem):
+    window = like.at[pl.ds(0, blocks)]
+    sem = recv_sem if send_sem is None else send_sem
+    copy = copy_to(axis, lax.rem(me + 1, count), window, window, sem, sem)
+    if send_sem is None:
+        copy.wait_recv()
+    else:
+        copy.wait_send()
 
 
 def join_pairs(read, write):
@@ -248,17 +235,18 @@
 
 def step_kernel(
     images_hbm, w_hbm, bias_hbm, gain_hbm, head_hbm, proj_hbm, text_hbm,
-    gimg_hbm, small_out, proj_out, gtext_out,
+    gimg, taps_out, bias_out, block_out, head_out, loss_out, proj_out, gtext_out,
     images, w_in, bias_in, gain_in, head_in, proj_in, text_in,
     pack, held, full, z, inv, zsum, sums, isum, pooled,
     normed_s, normed_r, part_s, part_r, img_s, img_r, row_s, row_r, dimg_s, dimg_r,
     demb_s, demb_r, dn_s, dn_r, text_s, text_r, col_s, col_r, dcap_s, dcap_r,
-    dnormed, projgrad, grads, dh, dn, mean1, gimg, blocks_s, blocks_r,
+    dnormed, projgrad, grads, dh, dn, mean1, blocks_s, mate_r, chip_s, chip_r,
     small, proj_r, small_r, proj_mine, small_mine, proj_all, small_all,
-    load_sem, fs, fr, ds, dr, ps, pr, ss, sr, gs, gr,
+    load_sem, fs, fr, ds, dr, ps, pr, ss, sr, gs, gr, hs, hr, near_s, near_r, far_s, far_r,
 ):
     me_f, me_d = lax.axis_index("fsdp"), lax.axis_index("dp")
-    my_pair = lax.div(me_f, 2)
+    my_pair, core = lax.div(me_f, 2), lax.rem(me_f, 2)
+    mate = 2 * my_pair + 1 - core
     greet(me_f, me_d)
     loads = [
         pltpu.make_async_copy(src, dst, load_sem.at[n])
@@ -293,23 +281,41 @@
     text_s[...] = text_unit
     text_r[me_d] = text_unit
     greeted()
-    x_pack = fex(7, lambda peer: pack, held)
-    x_pack.start()
+
+    def near_copy(p, block, dst):
+        return copy_to("fsdp", mate, block, dst, near_s, near_r.at[p])
+
+    def far_copy(t, n, block, dst):
+        q = lax.rem(my_pair + t, PAIRS)
+        return copy_to("fsdp", 2 * q + core, block, dst, far_s.at[n], far_r.at[n, my_pair])
+
+    near_copy(my_pair, pack, held.at[me_f]).start()
+    loop(1, PAIRS, lambda t: far_copy(t, 0, pack, held.at[me_f]).start())
     x_text = dex(0, lambda peer: text_s, text_r)
     x_text.start()
     for load in loads[4:]:
         load.wait()
 
+    def hand_on(t):
+        p = lax.rem(my_pair - t + PAIRS, PAIRS)
+        block = held.at[2 * p + core]
+        copy_to("fsdp", 2 * p + core, block, block, far_s.at[0], far_r.at[0, p]).wait_recv()
+        near_copy(p, block, block).start()
+
     def forward_pair(t):
         p = lax.rem(my_pair - t + PAIRS, PAIRS)
-        for c in range(2):
-
-            @pl.when(2 * p + c != me_f)
-            def _():
-                x_pack.wait_recv_from(2 * p + c)
-
+        block = held.at[2 * p + 1 - core]
+        near_copy(p, block, block).wait_recv()
         full[:, pair_lanes(p)] = jnp.concatenate([held[2 * p], held[2 * p + 1]], axis=1)
         loop(0, 3, lambda k: forward_block(3 * p + k, images, full, z, sums, isum))
+
+        @pl.when(t == 0)
+        def _():
+            hand_on(1)
+
+        @pl.when(t + 2 < PAIRS)
+        def _():
+            hand_on(t + 2)
 
     loop(0, PAIRS, forward_pair)
     pool_normed, pool_inverse = forward_norm(full, z, inv, zsum, sums, isum, pooled)
@@ -424,15 +430,15 @@
 
     def peers(act):
         def body(t):
-            act(t, lax.rem(me_d + t, N_DP))
-
-        loop(1, N_DP, body)
+            act(t, lax.rem(me_d + 1 + lax.rem(t + 11, N_DP - 1), N_DP))
+
+        loop(0, N_DP - 1, body)
 
     def proj_copy(t, peer, to):
-        return copy_to("dp", peer, projgrad.at[proj_rows(to)], proj_r.at[me_d], ps.at[t], pr.at[me_d])
+        return copy_to("dp", peer, projgrad.at[proj_rows(to)], proj_r.at[me_d], ps, pr)
 
     def small_copy(t, peer, to):
-        return copy_to("dp", peer, small.at[small_rows(to)], small_r.at[me_d], ss.at[t], sr.at[me_d])
+        return copy_to("dp", peer, small.at[small_rows(to)], small_r.at[me_d], ss, sr)
 
     def start_proj(t, peer):
         @pl.when(peer < first)
@@ -461,7 +467,9 @@
     dn[...] = d_norm
     grads[ROWS - 8 :, :] = jnp.zeros((8, CHANNELS), F32)
     grads[BLOCK_ROW : BLOCK_ROW + 1, :] = jnp.sum(d_hidden * zsum[...], axis=0, keepdims=True)
-    grads[LOSS_ROW : LOSS_ROW + 1, :] = jnp.full((1, CHANNELS), loss_part, F32)
+    grads[LOSS_ROW : LOSS_ROW + 1, :] = jnp.full(
+        (1, CHANNELS), loss_part * (0.5 / (N_DP * N_FSDP * IMGS)), F32
+    )
     mean1[...] = jnp.broadcast_to(jnp.mean(d_norm, axis=1, keepdims=True), mean1.shape)
     sums[...] = jnp.zeros_like(sums)
 
@@ -476,42 +484,47 @@
     mean2 = jnp.sum(sums[...], axis=3, keepdims=True) * (1.0 / CHANNELS)
     sums[...] = jnp.broadcast_to(mean2, sums.shape)
 
-    def block_copy(owner):
+    def mate_copy(p):
         return copy_to(
-            "fsdp", owner, blocks_s.at[owner], blocks_r.at[me_f], fs.at[8, owner], fr.at[8, me_f]
+            "fsdp", mate, blocks_s.at[2 * p + 1 - core], mate_r.at[p], hs, hr.at[p]
         )
+
+    def chip_sum(p):
+        copy_to("fsdp", mate, mate_r.at[p], mate_r.at[p], hs, hr.at[p]).wait_recv()
+        return blocks_s[2 * p + core] + mate_r[p]
+
+    def send_chip(t):
+        p = lax.rem(my_pair + t, PAIRS)
+        chip_s[p] = chip_sum(p)
+        far_copy(t, 1, chip_s.at[p], chip_r.at[my_pair]).start()
 
     def backward_pair(t):
         p = lax.rem(my_pair + t, PAIRS)
-        loop(
-            0, 3,
-            lambda k: backward_block(
-                3 * p + k, images, z, inv, full, dh, dn, sums, mean1, grads, gimg
-            ),
-        )
+
+        def piece(k):
+            backward_block(3 * p + k, images, z, inv, full, dh, dn, sums, mean1, grads, gimg)
+
+            @pl.when((k == 0) & (t > 1))
+            def _():
+                send_chip(t - 1)
+
+        loop(0, 3, piece)
         value = grads[:, pair_lanes(p)]
-        for c in range(2):
-            owner = 2 * p + c
-            blocks_s[owner] = value[:, SHARD * c : SHARD * (c + 1)]
-
-            @pl.when(owner != me_f)
-            def _():
-                block_copy(owner).start()
+        blocks_s[2 * p] = value[:, :SHARD]
+        blocks_s[2 * p + 1] = value[:, SHARD:]
+        mate_copy(p).start()
 
     loop(1, PAIRS + 1, backward_pair)
-    store = pltpu.make_async_copy(gimg, gimg_hbm, load_sem.at[7])
-    store.start()
-    blocks_r[me_f] = blocks_s[me_f]
-
-    def senders(act):
-        loop(1, N_FSDP, lambda t: act(lax.rem(me_f - t + N_FSDP, N_FSDP)))
-
-    senders(
-        lambda s: copy_to(
-            "fsdp", s, blocks_s.at[s], blocks_r.at[s], fs.at[8, s], fr.at[8, s]
+    chip_r[my_pair] = chip_sum(my_pair)
+
+    def chip_wait(t):
+        p = lax.rem(my_pair + t, PAIRS)
+        copy_to(
+            "fsdp", 2 * p + core, chip_r.at[p], chip_r.at[p], far_s.at[1], far_r.at[1, p]
         ).wait_recv()
-    )
-    small[...] = total(blocks_r, N_FSDP)
+
+    loop(1, PAIRS, chip_wait)
+    small[...] = total(chip_r, PAIRS)
     small[HEAD_ROW : HEAD_ROW + 1, :] = head_grad
 
     def start_small(t, peer):
@@ -521,38 +534,35 @@
 
     peers(start_small)
 
-    def all_copy(t, peer, sender, mine, everyone, slot):
-        return copy_to("dp", peer, mine, everyone.at[slot], gs.at[t], gr.at[sender])
-
-    @pl.when(me_d < first)
+    def proj_all_copy(peer):
+        return copy_to("dp", peer, proj_mine, proj_all.at[me_d], gs.at[0], gr.at[0])
+
+    def small_all_copy(peer):
+        return copy_to("dp", peer, small_mine, small_all.at[me_d - first], gs.at[1], gr.at[1])
+
+    def dp_wait(like, blocks, send_sem, recv_sem):
+        wait_blocks("dp", N_DP, me_d, like, blocks, send_sem, recv_sem)
+
+    owns_proj = me_d < first
+    owns_small = (me_d >= first) & (me_d < last)
+
+    @pl.when(owns_proj)
     def _():
         proj_r[me_d] = projgrad[proj_rows(me_d), :]
-
-        def wait(t, peer):
-            copy_to(
-                "dp", peer, projgrad.at[proj_rows(0)], proj_r.at[peer], ps.at[t], pr.at[peer]
-            ).wait_recv()
-
-        peers(wait)
+        dp_wait(proj_r, N_DP - 1, None, pr)
         out = total(proj_r, N_DP).astype(BF16)
         proj_mine[...] = out
         proj_all[me_d] = out
-        peers(lambda t, peer: all_copy(t, peer, me_d, proj_mine, proj_all, me_d).start())
-
-    @pl.when((me_d >= first) & (me_d < last))
+        peers(lambda t, peer: proj_all_copy(peer).start())
+
+    @pl.when(owns_small)
     def _():
         small_r[me_d] = small[small_rows(me_d), :]
-
-        def wait(t, peer):
-            copy_to(
-                "dp", peer, small.at[small_rows(first)], small_r.at[peer], ss.at[t], sr.at[peer]
-            ).wait_recv()
-
-        peers(wait)
+        dp_wait(small_r, N_DP - 1, None, sr)
         out = total(small_r, N_DP)
         small_mine[...] = out
         small_all[me_d - first] = out
-        peers(lambda t, peer: all_copy(t, peer, me_d, small_mine, small_all, me_d - first).start())
+        peers(lambda t, peer: small_all_copy(peer).start())
 
     x_dcap.wait_recv()
     d_caption = 7.0 * total(dcap_r, N_DP)
@@ -560,48 +570,60 @@
         d_caption - text_f * jnp.sum(text_f * d_caption, axis=1, keepdims=True)
     )
 
-    def wait_all(t, peer):
-        @pl.when(peer < first)
-        def _():
-            all_copy(t, peer, peer, proj_mine, proj_all, peer).wait_recv()
-
-        @pl.when((peer >= first) & (peer < last))
-        def _():
-            all_copy(t, peer, peer, small_mine, small_all, peer - first).wait_recv()
-
-    peers(wait_all)
+    for ex in (x_text, x_norm, x_part, x_img, x_col, x_row, x_dimg, x_dcap, x_demb, x_dn):
+        ex.wait_send()
+    wait_blocks("fsdp", N_FSDP, me_f, held, PAIRS, near_s, None)
+    wait_blocks("fsdp", N_FSDP, me_f, held, PAIRS - 1, far_s.at[0], None)
+    wait_blocks("fsdp", N_FSDP, me_f, mate_r, PAIRS, hs, None)
+    wait_blocks("fsdp", N_FSDP, me_f, chip_r, PAIRS - 1, far_s.at[1], None)
+
+    @pl.when(owns_proj)
+    def _():
+        dp_wait(proj_r, PROJ_OWNERS - 1, ps, None)
+        dp_wait(proj_all, PROJ_OWNERS - 1, None, gr.at[0])
+
+    @pl.when(me_d >= first)
+    def _():
+        dp_wait(proj_r, PROJ_OWNERS, ps, None)
+        dp_wait(proj_all, PROJ_OWNERS, None, gr.at[0])
+
     for k in range(PROJ_OWNERS):
         proj_out[8 * k : 8 * (k + 1), :] = proj_all[k].astype(F32)
-    for k in range(SMALL_OWNERS):
-        small_out[8 * k : 8 * (k + 1), :] = small_all[k]
-
-    store.wait()
-    for ex in (x_pack, x_text, x_norm, x_part, x_img, x_col, x_row, x_dimg, x_dcap, x_demb, x_dn):
-        ex.wait_send()
-
-    def drain_block(owner):
-        block_copy(owner).wait_send()
-
-    senders(drain_block)
-
-    def drain(t, peer):
-        @pl.when(peer < first)
-        def _():
-            proj_copy(t, peer, peer).wait_send()
-
-        @pl.when((peer >= first) & (peer < last))
-        def _():
-            small_copy(t, peer, peer).wait_send()
-
-        @pl.when(me_d < first)
-        def _():
-            all_copy(t, peer, me_d, proj_mine, proj_all, me_d).wait_send()
-
-        @pl.when((me_d >= first) & (me_d < last))
-        def _():
-            all_copy(t, peer, me_d, small_mine, small_all, me_d - first).wait_send()
-
-    peers(drain)
+
+    @pl.when(owns_small)
+    def _():
+        dp_wait(small_r, SMALL_OWNERS - 1, ss, None)
+        dp_wait(small_all, SMALL_OWNERS - 1, None, gr.at[1])
+        dp_wait(small_r, N_DP - 1, gs.at[1], None)
+
+    @pl.when((me_d < first) | (me_d >= last))
+    def _():
+        dp_wait(small_r, SMALL_OWNERS, ss, None)
+        dp_wait(small_all, SMALL_OWNERS, None, gr.at[1])
+
+    for k in range(BIAS_ROW // 8):
+        taps_out[8 * k : 8 * (k + 1), :] = small_all[k]
+    rest = small_all[BIAS_ROW // 8]
+    taps_out[BIAS_ROW - 1 :, :] = rest[:1]
+    bias_out[...] = rest[BIAS_ROW - 48 : BIAS_ROW - 47]
+    block_out[...] = rest[BLOCK_ROW - 48 : BLOCK_ROW - 47]
+    head_out[...] = rest[HEAD_ROW - 48 : HEAD_ROW - 47]
+    loss_out[...] = rest[LOSS_ROW - 48 : LOSS_ROW - 47, :128]
+
+    @pl.when(owns_proj)
+    def _():
+        wait_blocks("dp", N_DP, me_d, proj_all, N_DP - 1, gs.at[0], None)
+
+
+def store_kernel(*refs):
+    count = (len(refs) - 1) // 2
+    copies = [
+        pltpu.make_async_copy(refs[n], refs[count + n], refs[-1].at[n]) for n in range(count)
+    ]
+    for copy in copies:
+        copy.start()
+    for copy in copies:
+        copy.wait()
 
 
 def dma(*shape):
@@ -622,14 +644,20 @@
         return V((N_DP,) + shape, kind)
 
     inputs = (images, dw_weight, dw_bias[None], block_gain[None], head_gain[None], projection, text)
-    grad_images, sums, sum_proj, grad_text = pl.pallas_call(
+    inputs = [pltpu.with_memory_space_constraint(value, pltpu.HBM) for value in inputs]
+    row = (1, SHARD)
+    outs = [
+        jax.ShapeDtypeStruct(shape, kind)
+        for shape, kind in (
+            (maps, BF16), ((KERNEL * KERNEL, SHARD), F32), (row, F32), (row, F32), (row, F32),
+            ((1, 128), F32), ((SHARD, EMBED), F32), (two, F32),
+        )
+    ]
+    results = pl.pallas_call(
         step_kernel,
-        out_shape=[
-            jax.ShapeDtypeStruct(shape, kind)
-            for shape, kind in ((maps, BF16), ((ROWS, SHARD), F32), ((SHARD, EMBED), F32), (two, F32))
-        ],
-        in_specs=[pl.BlockSpec(memory_space=pl.ANY)] * len(inputs),
-        out_specs=[pl.BlockSpec(memory_space=pl.ANY)] + [VMEM_SPEC] * 3,
+        out_shape=outs,
+        in_specs=[pl.BlockSpec(memory_space=pltpu.HBM)] * len(inputs),
+        out_specs=[VMEM_SPEC] * len(outs),
         scratch_shapes=[
             V(maps, BF16), V((KERNEL * KERNEL, SHARD), F32), V((1, SHARD), F32), V((1, SHARD), F32),
             V((1, SHARD), F32), V((SHARD, EMBED), BF16), V(two, BF16),
@@ -647,28 +675,27 @@
             V((1, 128), F32), d_blocks((1, 128), F32),
             d_blocks(two, F32), d_blocks(two, F32),
             V(wide, F32), V((SHARD, EMBED), F32), V((ROWS, CHANNELS), F32), V(wide, F32),
-            V(wide, F32), V((IMGS, 128), F32), V(maps, BF16),
-            f_blocks((ROWS, SHARD), F32), f_blocks((ROWS, SHARD), F32),
+            V(wide, F32), V((IMGS, 128), F32), f_blocks((ROWS, SHARD), F32),
+            V((PAIRS, ROWS, SHARD), F32), V((PAIRS, ROWS, SHARD), F32), V((PAIRS, ROWS, SHARD), F32),
             V((ROWS, SHARD), F32), d_blocks((8, EMBED), F32), d_blocks((8, SHARD), F32),
             V((8, EMBED), BF16), V((8, SHARD), F32),
-            V((PROJ_OWNERS, 8, EMBED), BF16), V((SMALL_OWNERS, 8, SHARD), F32),
-            dma(8), dma(9, N_FSDP), dma(9, N_FSDP), dma(3, N_DP), dma(3, N_DP),
-            dma(N_DP), dma(N_DP), dma(N_DP), dma(N_DP), dma(N_DP), dma(N_DP),
+            d_blocks((8, EMBED), BF16), V((SMALL_OWNERS, 8, SHARD), F32),
+            dma(7), dma(7), dma(7), dma(3), dma(3), dma(), dma(), dma(), dma(), dma(2), dma(2),
+            dma(), dma(PAIRS), dma(), dma(PAIRS), dma(2), dma(2, PAIRS),
         ],
         compiler_params=pltpu.CompilerParams(
             vmem_limit_bytes=48 * 1024 * 1024, collective_id=0, has_side_effects=True
         ),
     )(*inputs)
-    return (
-        sums[LOSS_ROW, 0] / (2.0 * N_DP * N_FSDP * IMGS),
-        grad_images,
-        sums[: KERNEL * KERNEL],
-        sums[BIAS_ROW],
-        sums[BLOCK_ROW],
-        sums[HEAD_ROW],
-        sum_proj,
-        grad_text,
-    )
+    grad_images, taps, bias, block, head, loss, sum_proj, grad_text = pl.pallas_call(
+        store_kernel,
+        out_shape=outs,
+        in_specs=[VMEM_SPEC] * len(outs),
+        out_specs=[pl.BlockSpec(memory_space=pltpu.HBM)] * len(outs),
+        scratch_shapes=[dma(len(outs))],
+        compiler_params=pltpu.CompilerParams(vmem_limit_bytes=1024 * 1024),
+    )(*results)
+    return (loss[0, 0], grad_images, taps, bias[0], block[0], head[0], sum_proj, grad_text)
 
 
 def solution(mesh):

time: 132 us -> 116 us (0.88)
  the two profiles are of different devices: /device:TPU:33 before, /device:TPU:6 now
where the time goes in v4:
time: 116 us; the launch traced here: 115 us
  Pallas kernels  114 us (98%)
    pallas_call x1, Pallas kernels, local(): pl.pallas_call(step_kernel, out_shape=outs, in_specs=[pl.BlockSpec(memory...  113 us

profile of v4, /device:TPU:6, one launch (start us, length us, event | category | flops | bytes accessed | tf_op | source)
XLA Modules:
  0.0 115.1 jit_solution(6606753371809291040)
XLA Ops:
  0.6 113.3 %shard_map.134 = (bf16[2,8,8,3072]{3,2,1,0:T(8,128)(2,1)S(1)}, f32[49,192]{1,0:T(8,128)S(1)}, f32[1,192]{1,0:T(1,128)S(1)}, f32[1,192]{1,0:T(1,128)S(1)}, f32[1,...) custom-call(bf16[2,8,8,3072]{3,2,1,0:T(8,128)(2,1)} %images_hbm.1, ...), custom_call_target="tpu_custom_call" | custom-call | tf_op jit(solution)/shard_map/pallas_call | solution.py:656
  114.0 1.1 shard_map.135

commit v5 on v4

--- a/solution.py
+++ b/solution.py
@@ -124,6 +124,22 @@
 
 def pair_lanes(p):
     return pl.ds(pl.multiple_of(p * (2 * SHARD), 128), 2 * SHARD)
+
+
+DENSE, TAKEN = 40, KERNEL * KERNEL + 2
+
+
+def dense(rows):
+    rest = rows[DENSE:]
+    spare = [rest[:, 64 * n : 64 * (n + 1)] for n in range(3)]
+    spare.append(jnp.zeros((DENSE - 3 * (TAKEN - DENSE), 64), F32))
+    return jnp.concatenate([rows[:DENSE], jnp.concatenate(spare, axis=0)], axis=1)
+
+
+def rest_of(block):
+    count = TAKEN - DENSE
+    spare = block[:, SHARD:]
+    return jnp.concatenate([spare[count * n : count * (n + 1)] for n in range(3)], axis=1)
 
 
 def stack(ref, count):
@@ -215,19 +231,21 @@
             acc.append(hidden)
     grads[pl.ds(BIAS_ROW, 1), lanes] = jnp.sum(bias, axis=0, keepdims=True)
     for s in range(KERNEL):
-        cols = [shifted(value, s - margin) for value in maps]
-        for r in range(KERNEL):
-            tap = jnp.broadcast_to(full[pl.ds(r * KERNEL + s, 1), lanes], (MAP_SIDE, 128))
-            grad = None
-            for b in range(IMGS):
+        grad = [None] * KERNEL
+        for b in range(IMGS):
+            own = range(b * MAP_SIDE, (b + 1) * MAP_SIDE)
+            cols = [shifted(maps[k], s - margin) for k in own]
+            for r in range(KERNEL):
+                tap = jnp.broadcast_to(full[pl.ds(r * KERNEL + s, 1), lanes], (MAP_SIDE, 128))
                 for i in range(MAP_SIDE):
                     if 0 <= i - r + margin < MAP_SIDE:
-                        col = cols[b * MAP_SIDE + i - r + margin]
-                        k = b * MAP_SIDE + i
+                        col = cols[i - r + margin]
+                        k = own[i]
                         acc[k] = acc[k] + col * tap
                         term = col * pixels[k]
-                        grad = term if grad is None else grad + term
-            grads[pl.ds(r * KERNEL + s, 1), lanes] = jnp.sum(grad, axis=0, keepdims=True)
+                        grad[r] = term if grad[r] is None else grad[r] + term
+        for r in range(KERNEL):
+            grads[pl.ds(r * KERNEL + s, 1), lanes] = jnp.sum(grad[r], axis=0, keepdims=True)
     for b in range(IMGS):
         for i in range(MAP_SIDE):
             gimg[b, i, :, lanes] = acc[b * MAP_SIDE + i].astype(BF16)
@@ -269,9 +287,7 @@
     sums[...] = jnp.zeros_like(sums)
     for load in loads[:4]:
         load.wait()
-    rows = jnp.concatenate(
-        [w_in[...], bias_in[...], gain_in[...], jnp.zeros((ROWS - 51, SHARD), F32)], axis=0
-    )
+    rows = dense(jnp.concatenate([w_in[...], bias_in[...], gain_in[...]], axis=0))
     pack[...] = rows
     held[me_f] = rows
     text = text_in[...].astype(F32)
@@ -306,7 +322,9 @@
         p = lax.rem(my_pair - t + PAIRS, PAIRS)
         block = held.at[2 * p + 1 - core]
         near_copy(p, block, block).wait_recv()
-        full[:, pair_lanes(p)] = jnp.concatenate([held[2 * p], held[2 * p + 1]], axis=1)
+        left, right = held[2 * p], held[2 * p + 1]
+        full[:DENSE, pair_lanes(p)] = jnp.concatenate([left[:, :SHARD], right[:, :SHARD]], axis=1)
+        full[DENSE:TAKEN, pair_lanes(p)] = jnp.concatenate([rest_of(left), rest_of(right)], axis=1)
         loop(0, 3, lambda k: forward_block(3 * p + k, images, full, z, sums, isum))
 
         @pl.when(t == 0)
@@ -484,6 +502,47 @@
     mean2 = jnp.sum(sums[...], axis=3, keepdims=True) * (1.0 / CHANNELS)
     sums[...] = jnp.broadcast_to(mean2, sums.shape)
 
+    owns_proj = me_d < first
+
+    def dp_wait(like, blocks, send_sem, recv_sem):
+        wait_blocks("dp", N_DP, me_d, like, blocks, send_sem, recv_sem)
+
+    my_z, my_x = lax.div(me_d, 2), lax.rem(me_d, 2)
+    n_z = N_DP // 2
+    z_owners = PROJ_OWNERS // 2
+
+    def proj_start():
+        def body(t):
+            offset = 1 + lax.rem(t + n_z // 2 - 3, n_z - 1)
+            to = 2 * lax.rem(my_z + offset, n_z) + my_x
+            copy_to("dp", to, proj_mine, proj_all.at[my_x, my_z], gs.at[0], gr.at[0]).start()
+
+        loop(0, n_z - 1, body)
+
+    def proj_window(x, blocks):
+        return proj_all.at[x, pl.ds(0, blocks)]
+
+    def proj_wait(x, blocks, send_sem, recv_sem):
+        window = proj_window(x, blocks)
+        sem = recv_sem if send_sem is None else send_sem
+        copy = copy_to("dp", me_d + 1 - 2 * my_x, window, window, sem, sem)
+        if send_sem is None:
+            copy.wait_recv()
+        else:
+            copy.wait_send()
+
+    def proj_hand_on():
+        window = proj_window(my_x, z_owners)
+        return copy_to("dp", me_d + 1 - 2 * my_x, window, window, gs.at[2], gr.at[2])
+
+    def sum_proj():
+        proj_r[me_d] = projgrad[proj_rows(me_d), :]
+        dp_wait(proj_r, N_DP - 1, None, pr)
+        out = total(proj_r, N_DP).astype(BF16)
+        proj_mine[...] = out
+        proj_all[my_x, my_z] = out
+        proj_start()
+
     def mate_copy(p):
         return copy_to(
             "fsdp", mate, blocks_s.at[2 * p + 1 - core], mate_r.at[p], hs, hr.at[p]
@@ -493,13 +552,19 @@
         copy_to("fsdp", mate, mate_r.at[p], mate_r.at[p], hs, hr.at[p]).wait_recv()
         return blocks_s[2 * p + core] + mate_r[p]
 
+    def backward_order(t):
+        y, x = lax.div(my_pair, 2), lax.rem(my_pair, 2)
+        return 2 * lax.rem(y + 1 + lax.div(t - 1, 2), PAIRS // 2) + lax.rem(x + t, 2)
+
     def send_chip(t):
-        p = lax.rem(my_pair + t, PAIRS)
+        p = backward_order(t)
         chip_s[p] = chip_sum(p)
-        far_copy(t, 1, chip_s.at[p], chip_r.at[my_pair]).start()
+        copy_to(
+            "fsdp", 2 * p + core, chip_s.at[p], chip_r.at[my_pair], far_s.at[1], far_r.at[1, my_pair]
+        ).start()
 
     def backward_pair(t):
-        p = lax.rem(my_pair + t, PAIRS)
+        p = backward_order(t)
 
         def piece(k):
             backward_block(3 * p + k, images, z, inv, full, dh, dn, sums, mean1, grads, gimg)
@@ -534,26 +599,14 @@
 
     peers(start_small)
 
-    def proj_all_copy(peer):
-        return copy_to("dp", peer, proj_mine, proj_all.at[me_d], gs.at[0], gr.at[0])
-
     def small_all_copy(peer):
         return copy_to("dp", peer, small_mine, small_all.at[me_d - first], gs.at[1], gr.at[1])
 
-    def dp_wait(like, blocks, send_sem, recv_sem):
-        wait_blocks("dp", N_DP, me_d, like, blocks, send_sem, recv_sem)
-
-    owns_proj = me_d < first
-    owns_small = (me_d >= first) & (me_d < last)
-
     @pl.when(owns_proj)
     def _():
-        proj_r[me_d] = projgrad[proj_rows(me_d), :]
-        dp_wait(proj_r, N_DP - 1, None, pr)
-        out = total(proj_r, N_DP).astype(BF16)
-        proj_mine[...] = out
-        proj_all[me_d] = out
-        peers(lambda t, peer: proj_all_copy(peer).start())
+        sum_proj()
+
+    owns_small = (me_d >= first) & (me_d < last)
 
     @pl.when(owns_small)
     def _():
@@ -580,15 +633,15 @@
     @pl.when(owns_proj)
     def _():
         dp_wait(proj_r, PROJ_OWNERS - 1, ps, None)
-        dp_wait(proj_all, PROJ_OWNERS - 1, None, gr.at[0])
+        proj_wait(my_x, z_owners - 1, None, gr.at[0])
 
     @pl.when(me_d >= first)
     def _():
         dp_wait(proj_r, PROJ_OWNERS, ps, None)
-        dp_wait(proj_all, PROJ_OWNERS, None, gr.at[0])
-
-    for k in range(PROJ_OWNERS):
-        proj_out[8 * k : 8 * (k + 1), :] = proj_all[k].astype(F32)
+        proj_wait(my_x, z_owners, None, gr.at[0])
+
+    handed = proj_hand_on()
+    handed.start()
 
     @pl.when(owns_small)
     def _():
@@ -612,7 +665,12 @@
 
     @pl.when(owns_proj)
     def _():
-        wait_blocks("dp", N_DP, me_d, proj_all, N_DP - 1, gs.at[0], None)
+        proj_wait(0, n_z - 1, gs.at[0], None)
+
+    proj_wait(1 - my_x, z_owners, None, gr.at[2])
+    for k in range(PROJ_OWNERS):
+        proj_out[8 * k : 8 * (k + 1), :] = proj_all[k % 2, k // 2].astype(F32)
+    handed.wait_send()
 
 
 def store_kernel(*refs):
@@ -661,7 +719,7 @@
         scratch_shapes=[
             V(maps, BF16), V((KERNEL * KERNEL, SHARD), F32), V((1, SHARD), F32), V((1, SHARD), F32),
             V((1, SHARD), F32), V((SHARD, EMBED), BF16), V(two, BF16),
-            V((ROWS, SHARD), F32), f_blocks((ROWS, SHARD), F32), V((ROWS, CHANNELS), F32),
+            V((DENSE, 256), F32), f_blocks((DENSE, 256), F32), V((ROWS, CHANNELS), F32),
             V(maps, F32), V(lanes, F32), V(wide, F32), V(lanes, F32),
             V((IMGS, MAP_SIDE, CHANNELS), F32), V(wide, F32),
             f_blocks((IMGS, SHARD), F32), f_blocks((IMGS, SHARD), F32),
@@ -679,8 +737,8 @@
             V((PAIRS, ROWS, SHARD), F32), V((PAIRS, ROWS, SHARD), F32), V((PAIRS, ROWS, SHARD), F32),
             V((ROWS, SHARD), F32), d_blocks((8, EMBED), F32), d_blocks((8, SHARD), F32),
             V((8, EMBED), BF16), V((8, SHARD), F32),
-            d_blocks((8, EMBED), BF16), V((SMALL_OWNERS, 8, SHARD), F32),
-            dma(7), dma(7), dma(7), dma(3), dma(3), dma(), dma(), dma(), dma(), dma(2), dma(2),
+            V((2, N_DP // 2, 8, EMBED), BF16), V((SMALL_OWNERS, 8, SHARD), F32),
+            dma(7), dma(7), dma(7), dma(3), dma(3), dma(), dma(), dma(), dma(), dma(3), dma(3),
             dma(), dma(PAIRS), dma(), dma(PAIRS), dma(2), dma(2, PAIRS),
         ],
         compiler_params=pltpu.CompilerParams(

time: 116 us -> 113 us (0.974)
  Pallas kernels: 114 us -> 112 us
    pallas_call x1, Pallas kernels: 113 us -> 111 us  [local(): pl.pallas_call(step_kernel, out_shape=outs, in_specs=[pl.BlockSpec(memory...]
where the time goes in v5:
time: 113 us
  Pallas kernels  112 us (99%)
    pallas_call x1, Pallas kernels, local(): pl.pallas_call(step_kernel, out_shape=outs, in_specs=[pl.BlockSpec(memory...  111 us

profile of v5, /device:TPU:6, one launch (start us, length us, event | category | flops | bytes accessed | tf_op | source)
XLA Modules:
  0.0 112.8 jit_solution(11013446333814414468)
XLA Ops:
  0.6 111.0 %shard_map.134 = (bf16[2,8,8,3072]{3,2,1,0:T(8,128)(2,1)S(1)}, f32[49,192]{1,0:T(8,128)S(1)}, f32[1,192]{1,0:T(1,128)S(1)}, f32[1,192]{1,0:T(1,128)S(1)}, f32[1,...) custom-call(bf16[2,8,8,3072]{3,2,1,0:T(8,128)(2,1)} %images_hbm.1, ...), custom_call_target="tpu_custom_call" | custom-call | tf_op jit(solution)/shard_map/pallas_call | solution.py:714
  111.7 1.1 shard_map.135

commit v6 on v5

--- a/solution.py
+++ b/solution.py
@@ -49,6 +49,11 @@
     lax.fori_loop(low, high, step, 0)
 
 
+def far_first(count, far, body):
+    loop(far, count, body)
+    loop(1, far, body)
+
+
 def greet(me_f, me_d):
     barrier = pltpu.get_barrier_semaphore()
 
@@ -73,14 +78,13 @@
         self.source, self.dst, self.send_sem, self.recv_sem = source, dst, send_sem, recv_sem
 
     def start(self):
-        def body(t):
-            offset = 1 + lax.rem(t + self.count // 2 - 2, self.count - 1)
+        def body(offset):
             peer = lax.rem(self.me + offset, self.count)
             copy_to(
                 self.axis, peer, self.source(peer), self.dst.at[self.me], self.send_sem, self.recv_sem
             ).start()
 
-        loop(0, self.count - 1, body)
+        far_first(self.count, self.count // 2 - 1, body)
 
     def wait_recv(self):
         wait_blocks(self.axis, self.count, self.me, self.dst, self.count - 1, None, self.recv_sem)
@@ -447,10 +451,7 @@
         return pl.ds(pl.multiple_of((k - first) * 8, 8), 8)
 
     def peers(act):
-        def body(t):
-            act(t, lax.rem(me_d + 1 + lax.rem(t + 11, N_DP - 1), N_DP))
-
-        loop(0, N_DP - 1, body)
+        far_first(N_DP, 12, lambda offset: act(offset, lax.rem(me_d + offset, N_DP)))
 
     def proj_copy(t, peer, to):
         return copy_to("dp", peer, projgrad.at[proj_rows(to)], proj_r.at[me_d], ps, pr)
@@ -512,12 +513,11 @@
     z_owners = PROJ_OWNERS // 2
 
     def proj_start():
-        def body(t):
-            offset = 1 + lax.rem(t + n_z // 2 - 3, n_z - 1)
+        def body(offset):
             to = 2 * lax.rem(my_z + offset, n_z) + my_x
             copy_to("dp", to, proj_mine, proj_all.at[my_x, my_z], gs.at[0], gr.at[0]).start()
 
-        loop(0, n_z - 1, body)
+        far_first(n_z, n_z // 2 - 2, body)
 
     def proj_window(x, blocks):
         return proj_all.at[x, pl.ds(0, blocks)]

time: 113 us -> 113 us (level)
  no operation moved by 1% of the time
where the time goes in v6:
time: 113 us; the launch traced here: 112 us
  Pallas kernels  111 us (98%)
    pallas_call x1, Pallas kernels, local(): pl.pallas_call(step_kernel, out_shape=outs, in_specs=[pl.BlockSpec(memory...  110 us

profile of v6, /device:TPU:6, one launch (start us, length us, event | category | flops | bytes accessed | tf_op | source)
XLA Modules:
  0.0 112.1 jit_solution(5479390344160423842)
XLA Ops:
  0.6 110.3 %shard_map.134 = (bf16[2,8,8,3072]{3,2,1,0:T(8,128)(2,1)S(1)}, f32[49,192]{1,0:T(8,128)S(1)}, f32[1,192]{1,0:T(1,128)S(1)}, f32[1,192]{1,0:T(1,128)S(1)}, f32[1,...) custom-call(bf16[2,8,8,3072]{3,2,1,0:T(8,128)(2,1)} %images_hbm.1, ...), custom_call_target="tpu_custom_call" | custom-call | tf_op jit(solution)/shard_map/pallas_call | solution.py:714
  110.9 1.1 shard_map.135
